TPU v7x, 32 devices: a whole 2x2x4 slice. The times are simulated.
32 devices in a mesh: dp: 8 (over z, y), inner: 4 (over x, core).
Axes of the slice: x: 2, y: 2, z: 4, core: 2. Of those that a mesh axis runs over, the one named last changes fastest.
Arguments:
- tokens: bfloat16 [32768, 512], P(('dp', 'inner')), may hold values from -6 to 6
- segments: int32 [32768], P(('dp', 'inner')), may hold values from 0 to 32767, as said below
- positions: int32 [32768], P(('dp', 'inner')), may hold values from 0 to 1023, as said below
- cotangent: bfloat16 [32768, 512], P(('dp', 'inner')), may hold values from -6 to 6
- attn_weight: float32 [4, 512, 512], P(None, ('dp', 'inner')), may hold values from -0.53033009 to 0.53033009
- attn_m: float32 [4, 512, 512], P(None, ('dp', 'inner')), may hold values from -0.0007324219 to 0.0007324219
- attn_v: float32 [4, 512, 512], P(None, ('dp', 'inner')), may hold values from 1.0882435e-09 to 4.352974e-09
- gate_weight: float32 [2, 512, 512], P(None, ('dp', 'inner')), may hold values from -0.25 to 0.25
- gate_m: float32 [2, 512, 512], P(None, ('dp', 'inner')), may hold values from -0.00036621094 to 0.00036621094
- gate_v: float32 [2, 512, 512], P(None, ('dp', 'inner')), may hold values from 2.7206087e-10 to 1.0882435e-09
- in_weight: float32 [512, 2048], P(('dp', 'inner')), may hold values from -0.25 to 0.25
- in_m: float32 [512, 2048], P(('dp', 'inner')), may hold values from -0.00036621094 to 0.00036621094
- in_v: float32 [512, 2048], P(('dp', 'inner')), may hold values from 2.7206087e-10 to 1.0882435e-09
- out_weight: float32 [2048, 512], P(('dp', 'inner')), may hold values from -0.125 to 0.125
- out_m: float32 [2048, 512], P(('dp', 'inner')), may hold values from -0.00036621094 to 0.00036621094
- out_v: float32 [2048, 512], P(('dp', 'inner')), may hold values from 2.7206087e-10 to 1.0882435e-09
- norm_params: float32 [7, 512], P(None, ('dp', 'inner'))
- norm_m: float32 [7, 512], P(None, ('dp', 'inner')), may hold values from -0.0014648438 to 0.0014648438
- norm_v: float32 [7, 512], P(None, ('dp', 'inner')), may hold values from 4.352974e-09 to 1.7411896e-08
- in_bias: float32 [2048], P(('dp', 'inner')), may hold values from -1.75 to 1.75
- bias_m: float32 [2048], P(('dp', 'inner')), may hold values from -0.00024414062 to 0.00024414062
- bias_v: float32 [2048], P(('dp', 'inner')), may hold values from 1.7411896e-10 to 7.073583e-10
Outputs:
- layer_out: bfloat16 [32768, 512], P(('dp', 'inner'))
- input_grad: bfloat16 [32768, 512], P(('dp', 'inner'))
- grad_norm: float32 [], replicated
- attn_new: float32 [4, 512, 512], P(None, ('dp', 'inner'))
- attn_m_new: float32 [4, 512, 512], P(None, ('dp', 'inner'))
- attn_v_new: float32 [4, 512, 512], P(None, ('dp', 'inner'))
- gate_new: float32 [2, 512, 512], P(None, ('dp', 'inner'))
- gate_m_new: float32 [2, 512, 512], P(None, ('dp', 'inner'))
- gate_v_new: float32 [2, 512, 512], P(None, ('dp', 'inner'))
- in_new: float32 [512, 2048], P(('dp', 'inner'))
- in_m_new: float32 [512, 2048], P(('dp', 'inner'))
- in_v_new: float32 [512, 2048], P(('dp', 'inner'))
- out_new: float32 [2048, 512], P(('dp', 'inner'))
- out_m_new: float32 [2048, 512], P(('dp', 'inner'))
- out_v_new: float32 [2048, 512], P(('dp', 'inner'))
- norm_new: float32 [7, 512], P(None, ('dp', 'inner'))
- norm_m_new: float32 [7, 512], P(None, ('dp', 'inner'))
- norm_v_new: float32 [7, 512], P(None, ('dp', 'inner'))
- bias_new: float32 [2048], P(('dp', 'inner'))
- bias_m_new: float32 [2048], P(('dp', 'inner'))
- bias_v_new: float32 [2048], P(('dp', 'inner'))
Inputs may be any that keep to these rules, and one draw needn't show every extreme that they name: `segments`: a token's segment number is the index of its document's first token, so segment numbers never fall; a new document begins at every sequence start (every 1024 tokens); the first sequence is one document; the last token forms a document of its own. positions restart at 0 with every new segment number.
All inputs are finite; a program needn't handle non-finite values.
Results may differ from a plain program's by a relative error of at most 0.033.
The roundings to bfloat16 on the way count: a program that leaves them out, or rounds other values in their place, can miss the bound.
Values may be sent and summed in bfloat16 or wider, within the bound.
No kernel may reach another device: no remote copies, remote signals or barrier semaphores. Data moves between devices by JAX's collectives and lax.ppermute only.
A program may use at most 192 MiB of HBM per device.

v0:
```python
import functools
import jax
import jax.numpy as jnp
from jax import lax
from jax.experimental import pallas as pl
from jax.experimental.pallas import tpu as pltpu
from jax.sharding import PartitionSpec as P

AXES = ("dp", "inner")
HEADS = 8
HEAD = 64
STEP = 10
LOG2E = 1.4426950408889634
BLOCK = 256


norm_eps = 1e-05
first_decay = 0.9
second_decay = 0.999
adam_eps = 1e-08
learn_rate = 0.05
vector_rate = 0.8
weight_decay = 0.1
clip_norm = 1.0
masked_score = -1e30


def normalize_parts(values, gain_row, bias_row):
    centred = values - jnp.mean(values, -1, keepdims=True)
    spread = jnp.mean(centred * centred, -1, keepdims=True)
    scale_row = lax.rsqrt(spread + norm_eps)
    unit_rows = centred * scale_row
    return (unit_rows * gain_row + bias_row, unit_rows, scale_row)


def normalize_back(grad_rows, unit_rows, scale_row, gain_row):
    grad_unit = grad_rows * gain_row
    return scale_row * (
        grad_unit
        - jnp.mean(grad_unit, -1, keepdims=True)
        - unit_rows * jnp.mean(grad_unit * unit_rows, -1, keepdims=True)
    )


def bit_groups(sizes):
    dp_bits = sizes["dp"].bit_length() - 1
    inner_bits = sizes["inner"].bit_length() - 1
    y_bits = dp_bits // 2
    plane_bits = (inner_bits - 1) + y_bits
    return (1, plane_bits, dp_bits - y_bits)


def swap_with(array, offset, count):
    return lax.ppermute(array, AXES, [(source, source ^ offset) for source in range(count)])


def stage_bits(groups):
    return ((0, groups[0]), (groups[0], groups[1]), (groups[0] + groups[1], groups[2]))


def gather_z(shard, groups):
    count = 2 ** sum(groups)
    first_bit, bits = stage_bits(groups)[2]
    return jnp.stack([shard] + [swap_with(shard, offset << first_bit, count) for offset in range(1, 2**bits)])


def gather_plane(column, groups):
    count = 2 ** sum(groups)
    first_bit, bits = stage_bits(groups)[1]
    return [swap_with(column, offset << first_bit, count) for offset in range(1, 2**bits)]


def gather_core(column, planes, groups):
    return swap_with(jnp.concatenate([column] + planes), 1, 2 ** sum(groups))


def offsets_of(groups):
    (_, _), (plane_bit, plane_bits), (z_bit, z_bits) = stage_bits(groups)
    table = [
        [(plane << plane_bit) | (z << z_bit) for z in range(2**z_bits)] for plane in range(2**plane_bits)
    ]
    return table + [[offset | 1 for row in table for offset in row]]


def any_spec():
    return pl.BlockSpec(memory_space=pl.ANY)


def place_kernel(offsets, layout, own_ref, *refs):
    parts = refs[: len(offsets)]
    outs = refs[len(offsets) : len(offsets) + len(layout)]
    sems = refs[-1]
    own = own_ref[0]
    for part, row in zip(parts, offsets):
        for entry, offset in enumerate(row):
            owner = own ^ offset
            for index, (first, pieces) in enumerate(layout):
                pltpu.make_async_copy(
                    part.at[entry, first : first + pieces], outs[index].at[:, owner], sems.at[index]
                ).start()
    for index in range(len(layout)):
        pltpu.make_async_copy(outs[index], outs[index], sems.at[index]).wait()


def place(own, parts, layout, groups):
    count = 2 ** sum(groups)
    step, width = parts[0].shape[2:]
    offsets = offsets_of(groups)
    if step % 16:
        order = jnp.argsort(jnp.array([o for row in offsets for o in row]) ^ own)
        full = jnp.moveaxis(jnp.concatenate(parts)[order], 0, 1)
        return [full[first : first + pieces] for first, pieces in layout]
    return pl.pallas_call(
        functools.partial(place_kernel, offsets, layout),
        in_specs=[pl.BlockSpec(memory_space=pltpu.SMEM)] + [any_spec() for _ in parts],
        out_specs=[any_spec() for _ in layout],
        out_shape=[jax.ShapeDtypeStruct((pieces, count, step, width), jnp.bfloat16) for _, pieces in layout],
        scratch_shapes=[pltpu.SemaphoreType.DMA((len(layout),))],
        name="place",
    )(own[None].astype(jnp.int32), *parts)


def split_kernel(offsets, layout, own_ref, *refs):
    ins = refs[: len(layout)]
    kept, sent, sems = refs[len(layout) :]
    own = own_ref[0]
    for entry, offset in enumerate(offsets):
        for side, target in enumerate((kept, sent)):
            owner = own ^ (offset | side)
            for index, (first, pieces) in enumerate(layout):
                pltpu.make_async_copy(
                    ins[index].at[:, owner], target.at[entry, first : first + pieces], sems.at[side]
                ).start()
    pltpu.make_async_copy(kept, kept, sems.at[0]).wait()
    pltpu.make_async_copy(sent, sent, sems.at[1]).wait()


def split(own, grads, groups):
    step, width = grads[0].shape[2:]
    layout = []
    first = 0
    for grad in grads:
        layout.append((first, grad.shape[0]))
        first += grad.shape[0]
    offsets = [offset for row in offsets_of(groups)[:-1] for offset in row]
    if step % 16:
        full = jnp.moveaxis(jnp.concatenate(grads), 1, 0)
        order = jnp.array(offsets) ^ own
        return full[order], full[order ^ 1]
    shape = jax.ShapeDtypeStruct((len(offsets), first, step, width), jnp.bfloat16)
    return pl.pallas_call(
        functools.partial(split_kernel, offsets, layout),
        in_specs=[pl.BlockSpec(memory_space=pltpu.SMEM)] + [any_spec() for _ in grads],
        out_specs=[any_spec(), any_spec()],
        out_shape=[shape, shape],
        scratch_shapes=[pltpu.SemaphoreType.DMA((2,))],
        name="split",
    )(own[None].astype(jnp.int32), *grads)


def reduce_plane(kept, received, groups):
    count = 2 ** sum(groups)
    _, (first_bit, bits), (_, z_bits) = stage_bits(groups)
    shape = (2**bits, 2**z_bits) + kept.shape[1:]
    kept = kept.reshape(shape)
    received = received.reshape(shape)
    total = lambda offset: kept[offset].astype(jnp.float32) + received[offset].astype(jnp.float32)
    arrived = [
        swap_with(total(offset).astype(jnp.bfloat16), offset << first_bit, count) for offset in range(1, 2**bits)
    ]
    return total(0), arrived


def reduce_z(own_part, arrived, groups):
    count = 2 ** sum(groups)
    first_bit, bits = stage_bits(groups)[2]
    total = lambda z: own_part[z] + sum(part[z].astype(jnp.float32) for part in arrived)
    return total(0), [
        swap_with(total(z).astype(jnp.bfloat16), z << first_bit, count) for z in range(1, 2**bits)
    ]


def reduce_end(own_part, arrived):
    return own_part + sum(part.astype(jnp.float32) for part in arrived)


def sum_all(value, groups):
    for bit in range(sum(groups)):
        value = value + swap_with(value, 1 << bit, 2 ** sum(groups))
    return value


def tie(*values):
    return lax.optimization_barrier(values)


def small_rows(vec, bias, count, width):
    step = vec.shape[1] // count
    rows = jnp.concatenate(
        [vec.reshape(7, count, step).transpose(1, 0, 2).reshape(count, 7 * step), bias.reshape(count, 4 * step)], 1
    ).astype(jnp.bfloat16)
    return jnp.pad(rows, ((0, 0), (0, width - rows.shape[1])))


def small_back(rows, step):
    count = rows.shape[0]
    vec = rows[:, : 7 * step].reshape(count, 7, step).transpose(1, 0, 2).reshape(7, count * step)
    return vec, rows[:, 7 * step : 11 * step].reshape(-1)


def mat(a,b,dims):
    return lax.dot_general(a,b,(dims,((),())),preferred_element_type=jnp.float32)

def fill_bias(bias_ref, seg_col, pos_col, seg_row, pos_row):
    rows=bias_ref.shape[0]
    step=min(BLOCK,rows)
    for first in range(0,rows,step):
        sc=seg_col[first:first+step,:]; pc=pos_col[first:first+step,:]
        sr=seg_row[:,first:]; pr=pos_row[:,first:]
        allowed=(sc==sr)&(pc<=pr)
        bias_ref[first:first+step,first:]=jnp.where(allowed,0.0,masked_score)

def head_lanes(shape, which):
    lane=lax.broadcasted_iota(jnp.int32,shape,1)
    return (lane//HEAD)==which

def attn_fwd_kernel(segc,posc,segr,posr,q_ref,k_ref,v_ref,o_ref,lse_ref,bias_ref):
    @pl.when(pl.program_id(0)==0)
    def _():
        fill_bias(bias_ref,segc,posc,segr,posr)
    rows=q_ref.shape[0]; step=min(BLOCK,rows)
    pair=q_ref.shape[1]//HEAD
    const=HEAD**-0.5*LOG2E
    for first in range(0,rows,step):
        keys=first+step
        q=q_ref[first:keys,:]
        mixed=None
        for which in range(pair):
            own=head_lanes(q.shape,which)
            qh=jnp.where(own,q,jnp.zeros_like(q))
            s=mat(k_ref[:keys,:],qh,((1,),(1,)))*const+bias_ref[:keys,first:keys]
            m=jnp.max(s,0,keepdims=True)
            w=jnp.exp2(s-m)
            total=jnp.sum(w,0,keepdims=True)
            p=(w*(1.0/total)).astype(jnp.bfloat16)
            o=mat(p,v_ref[:keys,:],((0,),(0,)))
            mixed=o if mixed is None else jnp.where(own,o,mixed)
            lse_ref[0,which:which+1,first:keys]=m+jnp.log2(total)
        o_ref[first:keys,:]=mixed.astype(jnp.bfloat16)

def attn_bwd_kernel(segc,posc,segr,posr,q_ref,k_ref,v_ref,do_ref,lse_ref,dq_ref,dk_ref,dv_ref,bias_ref,dk_acc,dv_acc):
    @pl.when(pl.program_id(0)==0)
    def _():
        fill_bias(bias_ref,segc,posc,segr,posr)
    rows=q_ref.shape[0]; step=min(BLOCK,rows)
    pair=q_ref.shape[1]//HEAD
    const=HEAD**-0.5*LOG2E
    scale=HEAD**-0.5
    dk_acc[...]=jnp.zeros_like(dk_acc); dv_acc[...]=jnp.zeros_like(dv_acc)
    for first in range(0,rows,step):
        keys=first+step
        q=q_ref[first:keys,:]; do=do_ref[first:keys,:]
        dq=None
        for which in range(pair):
            own=head_lanes(q.shape,which)
            qh=jnp.where(own,q,jnp.zeros_like(q))
            doh=jnp.where(own,do,jnp.zeros_like(do))
            s=mat(k_ref[:keys,:],qh,((1,),(1,)))
            p=jnp.exp2(s*const+(bias_ref[:keys,first:keys]-lse_ref[0,which:which+1,first:keys]))
            dp=mat(v_ref[:keys,:],doh,((1,),(1,)))
            inner=jnp.sum(p*dp,0,keepdims=True)
            ds=(p*(dp-inner)).astype(jnp.bfloat16)
            dv_acc[:keys,:]+=mat(p.astype(jnp.bfloat16),doh,((1,),(0,)))
            dk_acc[:keys,:]+=mat(ds,qh,((1,),(0,)))
            d=mat(ds,k_ref[:keys,:],((0,),(0,)))
            dq=d if dq is None else jnp.where(own,d,dq)
        dq_ref[first:keys,:]=(dq*scale).astype(jnp.bfloat16)
    dk_ref[...]=(dk_acc[...]*scale).astype(jnp.bfloat16)
    dv_ref[...]=dv_acc[...].astype(jnp.bfloat16)

def const_map(*_): return (0,0)

def seg_args(segments,positions):
    return (segments[:,None],positions[:,None],segments[None],positions[None])

def attend(q,k,v,segments,positions):
    rows,width=q.shape
    pairs=width//128
    blk=pl.BlockSpec((rows,128),lambda j:(0,j))
    col=pl.BlockSpec((rows,1),const_map); row=pl.BlockSpec((1,rows),const_map)
    return pl.pallas_call(attn_fwd_kernel,grid=(pairs,),
        in_specs=[col,col,row,row,blk,blk,blk],
        out_specs=[blk,pl.BlockSpec((1,2,rows),lambda j:(j,0,0))],
        out_shape=[jax.ShapeDtypeStruct((rows,width),jnp.bfloat16),jax.ShapeDtypeStruct((pairs,2,rows),jnp.float32)],
        scratch_shapes=[pltpu.VMEM((rows,rows),jnp.float32)],
        name="attn_fwd",
    )(*seg_args(segments,positions),q,k,v)

def attend_back(q,k,v,do,lse,segments,positions,base,pairs):
    rows=q.shape[0]
    blk=pl.BlockSpec((rows,128),lambda j:(0,j+base))
    oblk=pl.BlockSpec((rows,128),lambda j:(0,j))
    col=pl.BlockSpec((rows,1),const_map); row=pl.BlockSpec((1,rows),const_map)
    out=jax.ShapeDtypeStruct((rows,128*pairs),jnp.bfloat16)
    return pl.pallas_call(attn_bwd_kernel,grid=(pairs,),
        in_specs=[col,col,row,row,blk,blk,blk,blk,pl.BlockSpec((1,2,rows),lambda j:(j+base,0,0))],
        out_specs=[oblk,oblk,oblk],
        out_shape=[out,out,out],
        scratch_shapes=[pltpu.VMEM((rows,rows),jnp.float32),pltpu.VMEM((rows,128),jnp.float32),pltpu.VMEM((rows,128),jnp.float32)],
        name="attn_bwd",
    )(*seg_args(segments,positions),q,k,v,do,lse)


def adam_update(weight, first_moment, second_moment, gradient, factor, step_rate):
    clipped = gradient * factor
    first_new = first_decay * first_moment + (1.0 - first_decay) * clipped
    second_new = second_decay * second_moment + (1.0 - second_decay) * clipped * clipped
    corrected = first_new / (1.0 - first_decay**STEP)
    spread = second_new / (1.0 - second_decay**STEP)
    weight_new = weight - step_rate * (
        corrected / (jnp.sqrt(spread) + adam_eps) + weight_decay * weight
    )
    return (weight_new, first_new, second_new)


def body(
    groups,
    tokens,
    segments,
    positions,
    cotangent,
    attn_weight,
    attn_m,
    attn_v,
    gate_weight,
    gate_m,
    gate_v,
    in_weight,
    in_m,
    in_v,
    out_weight,
    out_m,
    out_v,
    norm_params,
    norm_m,
    norm_v,
    in_bias,
    bias_m,
    bias_v,
):
    count = 2 ** sum(groups)
    own = lax.axis_index(AXES)
    width = 512
    step = attn_weight.shape[1]
    low = lambda value: value.astype(jnp.bfloat16)
    dot = functools.partial(jnp.einsum, preferred_element_type=jnp.float32)
    columns = lambda value: [value[:, width * j : width * (j + 1)] for j in range(4)]
    small = jnp.pad(small_rows(norm_params, in_bias, 1, width), ((0, step - 1), (0, 0)))
    first_shard = jnp.stack(
        [low(attn_weight[0]), low(attn_weight[1]), low(attn_weight[2]), low(gate_weight[0]), low(attn_weight[3]), small]
    )
    second_shard = jnp.concatenate(
        [
            jnp.stack([low(gate_weight[1])] + columns(low(in_weight))),
            low(out_weight).reshape(4, step, width),
        ]
    )
    z_first = gather_z(first_shard, groups)
    z_first, second_shard = tie(z_first, second_shard)
    plane_first = gather_plane(z_first, groups)
    z_second = gather_z(second_shard, groups)
    z_second, *plane_first = tie(z_second, *plane_first)
    core_first = gather_core(z_first, plane_first, groups)
    plane_second = gather_plane(z_second, groups)
    w_four, w_o, small_all = place(
        own, [z_first] + plane_first + [core_first], [(0, 4), (4, 1), (5, 1)], groups
    )
    w_four = w_four.reshape(4, count * step, width)
    w_o = w_o.reshape(count * step, width)
    vectors, bias = small_back(small_all[0, :, 0].astype(jnp.float32), step)
    inputs = tokens.astype(jnp.float32)
    normed_full, unit_one, scale_one = normalize_parts(inputs, vectors[0], vectors[1])
    normed = low(normed_full)
    queries, keys, values = [low(dot("td,de->te", normed, w_four[j])) for j in range(3)]
    mixed_heads, log_total = attend(queries, keys, values, segments, positions)
    mixed_heads, *plane_second = tie(mixed_heads, *plane_second)
    core_second = gather_core(z_second, plane_second, groups)
    attended = dot("td,de->te", mixed_heads, w_o)
    attn_gate = jax.nn.sigmoid(dot("td,de->te", normed, w_four[3]) + vectors[4])
    middle = attn_gate * attended + (1.0 - attn_gate) * inputs
    normed_two_full, unit_two, scale_two = normalize_parts(middle, vectors[2], vectors[3])
    normed_two = low(normed_two_full)
    w_f, w_in, w_out = place(
        own, [z_second] + plane_second + [core_second], [(0, 1), (1, 4), (5, 4)], groups
    )
    w_f = w_f.reshape(count * step, width)
    w_in = jnp.concatenate(list(w_in.reshape(4, count * step, width)), 1)
    w_out = w_out.transpose(1, 0, 2, 3).reshape(4 * count * step, width)
    hidden = dot("td,df->tf", normed_two, w_in) + bias
    active = low(jnp.maximum(hidden, 0.0))
    branch = dot("tf,fd->td", active, w_out) + vectors[6]
    ffn_gate = jax.nn.sigmoid(dot("td,de->te", normed_two, w_f) + vectors[5])
    layer_out = low(ffn_gate * branch + (1.0 - ffn_gate) * middle)
    grad_out = cotangent.astype(jnp.float32)
    grad_branch = grad_out * ffn_gate
    grad_fgate = grad_out * (branch - middle) * ffn_gate * (1.0 - ffn_gate)
    grad_middle = grad_out * (1.0 - ffn_gate)
    branch_low = low(grad_branch)
    grad_w_out = low(dot("tf,td->fd", active, branch_low))
    grad_active = dot("td,fd->tf", branch_low, w_out)
    grad_hidden = jnp.where(hidden > 0.0, grad_active, 0.0)
    hidden_low = low(grad_hidden)
    grad_w_in = low(dot("td,tf->df", normed_two, hidden_low))
    fgate_low = low(grad_fgate)
    grad_w_f = low(dot("td,te->de", normed_two, fgate_low))
    grad_normed_two = dot("tf,df->td", hidden_low, w_in) + dot("te,de->td", fgate_low, w_f)
    grad_gain_two = jnp.sum(grad_normed_two * unit_two, 0)
    grad_shift_two = jnp.sum(grad_normed_two, 0)
    grad_middle = grad_middle + normalize_back(grad_normed_two, unit_two, scale_two, vectors[2])
    grad_attended = grad_middle * attn_gate
    grad_agate = grad_middle * (attended - inputs) * attn_gate * (1.0 - attn_gate)
    grad_inputs = grad_middle * (1.0 - attn_gate)
    attended_low = low(grad_attended)
    grad_w_o = low(dot("td,te->de", mixed_heads, attended_low))
    grad_mixed = low(dot("te,de->td", attended_low, w_o))
    blocks = lambda value: value.reshape(-1, count, step, width)
    kept_b, sent_b = split(
        own,
        [
            blocks(grad_w_f),
            blocks(jnp.stack(columns(grad_w_in))),
            grad_w_out.reshape(count, 4, step, width).transpose(1, 0, 2, 3),
            blocks(grad_w_o),
        ],
        groups,
    )
    core_b = swap_with(sent_b, 1, count)
    half_one = attend_back(queries, keys, values, grad_mixed, log_total, segments, positions, 0, 2)
    core_b, kept_b, *half_one = tie(core_b, kept_b, *half_one)
    own_b, plane_b = reduce_plane(kept_b, core_b, groups)
    half_two = attend_back(queries, keys, values, grad_mixed, log_total, segments, positions, 2, 2)
    triple_grad = [jnp.concatenate([one, two], 1) for one, two in zip(half_one, half_two)]
    agate_low = low(grad_agate)
    back_four = triple_grad + [agate_low]
    grad_normed = sum(dot("te,de->td", back_four[j], w_four[j]) for j in range(4))
    grad_w_four = jnp.stack([low(dot("td,te->de", normed, back_four[j])) for j in range(4)])
    grad_gain_one = jnp.sum(grad_normed * unit_one, 0)
    grad_shift_one = jnp.sum(grad_normed, 0)
    grad_inputs = grad_inputs + normalize_back(grad_normed, unit_one, scale_one, vectors[0])
    input_grad = low(grad_inputs)
    grad_vectors = jnp.stack(
        [
            grad_gain_one,
            grad_shift_one,
            grad_gain_two,
            grad_shift_two,
            jnp.sum(grad_agate, 0),
            jnp.sum(grad_fgate, 0),
            jnp.sum(grad_branch, 0),
        ]
    )
    grad_bias = jnp.sum(grad_hidden, 0)
    grad_small = jnp.pad(small_rows(grad_vectors, grad_bias, count, width)[:, None], ((0, 0), (0, step - 1), (0, 0)))
    kept_a, sent_a = split(own, [blocks(grad_w_four), grad_small[None]], groups)
    kept_a, sent_a, *plane_b = tie(kept_a, sent_a, *plane_b)
    core_a = swap_with(sent_a, 1, count)
    own_b, z_b = reduce_z(own_b, plane_b, groups)
    own_a, plane_a = reduce_plane(kept_a, core_a, groups)
    own_a, z_a = reduce_z(own_a, plane_a, groups)
    total_b = reduce_end(own_b, z_b)
    total_a = reduce_end(own_a, z_a)
    own_small = total_a[4, :1]
    own_vec, own_bias = small_back(own_small, step)
    owned = (
        jnp.concatenate([total_a[:3], total_b[9:]]),
        jnp.stack([total_a[3], total_b[0]]),
        jnp.concatenate(list(total_b[1:5]), 1),
        total_b[5:9].reshape(4 * step, width),
        own_vec,
        own_bias,
    )
    local_squares = jnp.sum(total_b * total_b) + jnp.sum(total_a[:4] * total_a[:4]) + jnp.sum(own_small * own_small)
    grad_norm = jnp.sqrt(sum_all(local_squares, groups))
    factor = jnp.minimum(1.0, clip_norm / (grad_norm + 1e-06))
    states = (
        (attn_weight, attn_m, attn_v),
        (gate_weight, gate_m, gate_v),
        (in_weight, in_m, in_v),
        (out_weight, out_m, out_v),
        (norm_params, norm_m, norm_v),
        (in_bias, bias_m, bias_v),
    )
    step_rates = (learn_rate, learn_rate, learn_rate, learn_rate, vector_rate, vector_rate)
    updated = [
        adam_update(state[0], state[1], state[2], gradient, factor, step_rate)
        for state, gradient, step_rate in zip(states, owned, step_rates)
    ]
    return (
        layer_out,
        input_grad,
        grad_norm,
        updated[0][0],
        updated[0][1],
        updated[0][2],
        updated[1][0],
        updated[1][1],
        updated[1][2],
        updated[2][0],
        updated[2][1],
        updated[2][2],
        updated[3][0],
        updated[3][1],
        updated[3][2],
        updated[4][0],
        updated[4][1],
        updated[4][2],
        updated[5][0],
        updated[5][1],
        updated[5][2],
    )


def solution(mesh):
    return jax.shard_map(
        functools.partial(body, bit_groups(mesh.shape)),
        mesh=mesh,
        in_specs=(
            P(("dp", "inner"), None),
            P(("dp", "inner")),
            P(("dp", "inner")),
            P(("dp", "inner"), None),
            P(None, ("dp", "inner"), None),
            P(None, ("dp", "inner"), None),
            P(None, ("dp", "inner"), None),
            P(None, ("dp", "inner"), None),
            P(None, ("dp", "inner"), None),
            P(None, ("dp", "inner"), None),
            P(("dp", "inner"), None),
            P(("dp", "inner"), None),
            P(("dp", "inner"), None),
            P(("dp", "inner"), None),
            P(("dp", "inner"), None),
            P(("dp", "inner"), None),
            P(None, ("dp", "inner")),
            P(None, ("dp", "inner")),
            P(None, ("dp", "inner")),
            P(("dp", "inner")),
            P(("dp", "inner")),
            P(("dp", "inner")),
        ),
        out_specs=(
            P(("dp", "inner"), None),
            P(("dp", "inner"), None),
            P(),
            P(None, ("dp", "inner"), None),
            P(None, ("dp", "inner"), None),
            P(None, ("dp", "inner"), None),
            P(None, ("dp", "inner"), None),
            P(None, ("dp", "inner"), None),
            P(None, ("dp", "inner"), None),
            P(("dp", "inner"), None),
            P(("dp", "inner"), None),
            P(("dp", "inner"), None),
            P(("dp", "inner"), None),
            P(("dp", "inner"), None),
            P(("dp", "inner"), None),
            P(None, ("dp", "inner")),
            P(None, ("dp", "inner")),
            P(None, ("dp", "inner")),
            P(("dp", "inner")),
            P(("dp", "inner")),
            P(("dp", "inner")),
        ),
        check_vma=False,
    )
```

profile of v0, /device:TPU:0, one launch (start us, length us, event | category | flops | bytes accessed | tf_op | source)
XLA Modules:
  0.0 727.6 jit_solution(2652924128794558743)
XLA Ops:
  4.0 5.1 collective-permute-start.2
  12.9 4.6 collective-permute-done.1
  17.5 2.6 collective-permute-start.5
  20.1 1.5 collective-permute-start.6
  21.6 1.5 collective-permute-start.7
  23.6 1.7 collective-permute-done.5
  25.2 5.6 collective-permute-start.3
  32.1 1.8 collective-permute-done.3
  34.1 5.0 collective-permute-done.7.refs_2_
  45.6 1.4 collective-permute-start.12
  47.0 96.4 %place.2 = (bf16[4,32,16,512]{3,2,1,0:T(8,128)(2,1)}, bf16[1,32,16,512]{3,2,1,0:T(8,128)(2,1)}, bf16[1,32,16,512]{3,2,1,0:T(8,128)(2,1)}) custom-call(s32[1]{0:T(128)} %bitcast.own_ref, bf16[4,6,16,512]{3,2,1,0:T(8,128)(2,1)} %copy-done.10, bf16[4,6,16,512]{3,2,1,0:T(8,128)(2,1)} %copy-done.23, bf16[4,6,16,512]{3,2,1,0:T(8,128)(2,1)} %copy-done.24, ...), custom_call_target="tpu_custom_call" | custom-call | tf_op jit(solution)/shard_map/place/pallas_call | solution.py:113
  143.5 2.9 fusion.96
  149.8 2.9 convolution_convert_fusion.5.q_ref
  152.7 1.7 convolution_convert_fusion.4.k_ref
  154.4 1.9 convolution_convert_fusion.3.v_ref
  156.3 14.3 %attn_fwd.1 = (bf16[1024,512]{1,0:T(8,128)(2,1)}, f32[4,2,1024]{2,1,0:T(2,128)}) custom-call(s32[1024,1]{1,0:T(8,128)} %copy.86.segc, s32[1024,1]{1,0:T(8,128)} %copy.87.posc, s32[1,1024]{1,0:T(1,128)} %bitcast.199, s32[1,1024]{1,0:T(1,128)} %bitcast.203, bf16[1024,512]{1,0:T(8,128)(2,1)} %convolution_convert_fusion.5.q_ref, ...), custom_call_target="tpu_custom_call" | custom-call | tf_op jit(solution)/shard_map/attn_fwd/pallas_call | solution.py:291
  170.7 2.0 pad_maximum_fusion
  173.7 2.1 fusion.99
  175.8 2.8 fusion.92
  180.4 144.1 %place.3 = (bf16[1,32,16,512]{3,2,1,0:T(8,128)(2,1)}, bf16[4,32,16,512]{3,2,1,0:T(8,128)(2,1)}, bf16[4,32,16,512]{3,2,1,0:T(8,128)(2,1)}) custom-call(s32[1]{0:T(128)} %bitcast.own_ref, bf16[4,9,16,512]{3,2,1,0:T(8,128)(2,1)} %copy-done.8, bf16[4,9,16,512]{3,2,1,0:T(8,128)(2,1)} %copy-done.11, bf16[4,9,16,512]{3,2,1,0:T(8,128)(2,1)} %copy-done.12, ...), custom_call_target="tpu_custom_call" | custom-call | tf_op jit(solution)/shard_map/place/pallas_call | solution.py:113
  324.5 2.0 copy.91
  326.9 1.4 copy-done.4
  328.3 2.4 fusion.32
  330.8 2.3 fusion.27
  333.1 3.2 fusion.87
  336.3 4.4 fusion.98
  340.7 4.7 fusion.23
  345.4 2.6 convolution_convert_fusion.1
  347.9 2.4 convolution_convert_fusion
  350.3 1.9 convolution_convert_fusion.11
  352.3 1.4 multiply_reduce_fusion
  353.9 1.5 copy.104
  356.2 2.7 fusion.89
  361.0 1.5 convolution_convert_fusion.10
  362.5 1.6 pad_maximum_fusion.2.refs_1_
  364.1 159.9 %split.2 = (bf16[16,10,16,512]{3,2,1,0:T(8,128)(2,1)}, bf16[16,10,16,512]{3,2,1,0:T(8,128)(2,1)}) custom-call(s32[1]{0:T(128)} %bitcast.own_ref, bf16[1,32,16,512]{3,2,1,0:T(8,128)(2,1)} %bitcast.175, bf16[4,32,16,512]{3,2,1,0:T(8,128)(2,1)} %pad_maximum_fusion.2.refs_1_, bf16[4,32,16,512]{3,2,1,0:T(8,128)(2,1)} %bitcast.151, bf16[1,32,16,512]{3,2,1,0:T(8,128)(2,1)} %bitcast.184), custom_call_target="tpu_custom_call" | custom-call | tf_op jit(solution)/shard_map/split/pallas_call | solution.py:151
  524.5 3.1 convolution_convert_fusion.2.do_ref
  527.6 13.0 %attn_bwd.2 = (bf16[1024,256]{1,0:T(8,128)(2,1)}, bf16[1024,256]{1,0:T(8,128)(2,1)}, bf16[1024,256]{1,0:T(8,128)(2,1)}) custom-call(s32[1024,1]{1,0:T(8,128)} %copy.86.segc, s32[1024,1]{1,0:T(8,128)} %copy.87.posc, s32[1,1024]{1,0:T(1,128)} %bitcast.200, s32[1,1024]{1,0:T(1,128)} %bitcast.204, bf16[1024,512]{1,0:T(8,128)(2,1)} %convolution_convert_fusion.5.q_ref, ...), custom_call_target="tpu_custom_call" | custom-call | tf_op jit(solution)/shard_map/attn_bwd/pallas_call | solution.py:305
  540.7 13.2 %attn_bwd.3 = (bf16[1024,256]{1,0:T(8,128)(2,1)}, bf16[1024,256]{1,0:T(8,128)(2,1)}, bf16[1024,256]{1,0:T(8,128)(2,1)}) custom-call(s32[1024,1]{1,0:T(8,128)} %copy.86.segc, s32[1024,1]{1,0:T(8,128)} %copy.87.posc, s32[1,1024]{1,0:T(1,128)} %bitcast.201, s32[1,1024]{1,0:T(1,128)} %bitcast.205, bf16[1024,512]{1,0:T(8,128)(2,1)} %convolution_convert_fusion.5.q_ref, ...), custom_call_target="tpu_custom_call" | custom-call | tf_op jit(solution)/shard_map/attn_bwd/pallas_call | solution.py:305
  554.4 3.2 convolution_convert_fusion.6
  559.5 1.9 convolution_convert_fusion.7
  563.2 1.9 convolution_convert_fusion.8
  567.6 3.2 fusion.13
  571.2 5.2 add_convert_fusion.2
  578.5 1.4 collective-permute-start.17
  582.3 1.6 pad_maximum_fusion.3.refs_0_
  583.9 80.5 %split.3 = (bf16[16,5,16,512]{3,2,1,0:T(8,128)(2,1)}, bf16[16,5,16,512]{3,2,1,0:T(8,128)(2,1)}) custom-call(s32[1]{0:T(128)} %bitcast.own_ref, bf16[4,32,16,512]{3,2,1,0:T(8,128)(2,1)} %pad_maximum_fusion.3.refs_0_, bf16[1,32,16,512]{3,2,1,0:T(8,128)(2,1)} %pad_bitcast_fusion.refs_1_), custom_call_target="tpu_custom_call" | custom-call | tf_op jit(solution)/shard_map/split/pallas_call | solution.py:151
  664.6 2.1 fusion.38
  666.7 1.8 collective-permute-start.20
  668.5 2.6 collective-permute-start.18
  671.7 1.6 collective-permute-start.24
  677.0 1.9 fusion.12
  678.8 3.3 collective-permute-done.19
  682.1 2.0 multiply_reduce_fusion.5
  684.1 4.7 collective-permute-done.23
  689.1 1.8 collective-permute-start.27
  691.0 2.6 collective-permute-start.25
  693.6 2.7 collective-permute-done.27
  696.4 2.4 collective-permute-done.26
  703.9 2.6 collective-permute-start.29
  708.1 2.8 collective-permute-start.30
  713.7 2.2 collective-permute-done.31
  716.6 2.0 collective-permute-start.32
  718.5 2.5 collective-permute-done.32
  (273 shorter events, 51.5 us)
Async XLA Ops:
  4.0 8.8 %collective-permute-start.2 = (bf16[6,16,512]{2,1,0:T(8,128)(2,1)S(1)}, bf16[6,16,512]{2,1,0:T(8,128)(2,1)S(1)}, u32[]{:S(2)}, u32[]{:S(2)}) collective-permute-start(bf16[6,16,512]{2,1,0:T(8,128)(2,1)S(1)} %get-tuple-element.167), channel_id=1, source_target_pairs={{0,24},{1,25},{2,26},{3,27},{4,28},{5,29},{6,30},{7,31},{8,16},{9,... | collective-permute-start | bytes 294920 | tf_op jit(solution)/shard_map/ppermute | solution.py:54
  9.2 8.3 %collective-permute-start.1 = (bf16[6,16,512]{2,1,0:T(8,128)(2,1)S(1)}, bf16[6,16,512]{2,1,0:T(8,128)(2,1)S(1)}, u32[]{:S(2)}, u32[]{:S(2)}) collective-permute-start(bf16[6,16,512]{2,1,0:T(8,128)(2,1)S(1)} %get-tuple-element.167), channel_id=1, source_target_pairs={{0,16},{1,17},{2,18},{3,19},{4,20},{5,21},{6,22},{7,23},{8,24},{9,... | collective-permute-start | bytes 294920 | tf_op jit(solution)/shard_map/ppermute | solution.py:54
  9.2 8.3 %collective-permute-start = (bf16[6,16,512]{2,1,0:T(8,128)(2,1)S(1)}, bf16[6,16,512]{2,1,0:T(8,128)(2,1)S(1)}, u32[]{:S(2)}, u32[]{:S(2)}) collective-permute-start(bf16[6,16,512]{2,1,0:T(8,128)(2,1)S(1)} %get-tuple-element.167), channel_id=1, source_target_pairs={{0,8},{1,9},{2,10},{3,11},{4,12},{5,13},{6,14},{7,15},{8,0},{9,1},... | collective-permute-start | bytes 294920 | tf_op jit(solution)/shard_map/ppermute | solution.py:54
  17.5 23.1 %copy-start.10 = (bf16[4,6,16,512]{3,2,1,0:T(8,128)(2,1)}, bf16[4,6,16,512]{3,2,1,0:T(8,128)(2,1)S(1)}, u32[]{:S(2)}) copy-start(bf16[4,6,16,512]{3,2,1,0:T(8,128)(2,1)S(1)} %pad_maximum_fusion.6.refs_0_) | copy-start | bytes 1179652
  17.5 7.7 %collective-permute-start.5 = (bf16[9,16,512]{2,1,0:T(8,128)(2,1)S(1)}, bf16[9,16,512]{2,1,0:T(8,128)(2,1)S(1)}, u32[]{:S(2)}, u32[]{:S(2)}) collective-permute-start(bf16[9,16,512]{2,1,0:T(8,128)(2,1)S(1)} %constant_dynamic-update-slice_fusion), channel_id=1, source_target_pairs={{0,24},{1,25},{2,26},{3,27},{4,28},{5,29},{6,30},{7,31},{8,16},{9,... | collective-permute-start | bytes 442376 | tf_op jit(solution)/shard_map/ppermute | solution.py:54
  20.1 14.0 %collective-permute-start.6 = (bf16[4,6,16,512]{3,2,1,0:T(8,128)(2,1)S(1)}, bf16[4,6,16,512]{3,2,1,0:T(8,128)(2,1)S(1)}, u32[]{:S(2)}, u32[]{:S(2)}) collective-permute-start(bf16[4,6,16,512]{3,2,1,0:T(8,128)(2,1)S(1)} %pad_maximum_fusion.6.refs_0_), channel_id=1, source_target_pairs={{0,2},{1,3},{2,0},{3,1},{4,6},{5,7},{6,4},{7,5},{8,10},{9,11},{10,... | collective-permute-start | bytes 1179656 | tf_op jit(solution)/shard_map/ppermute | solution.py:54
  21.6 17.6 %collective-permute-start.7 = (bf16[4,6,16,512]{3,2,1,0:T(8,128)(2,1)S(1)}, bf16[4,6,16,512]{3,2,1,0:T(8,128)(2,1)S(1)}, u32[]{:S(2)}, u32[]{:S(2)}) collective-permute-start(bf16[4,6,16,512]{3,2,1,0:T(8,128)(2,1)S(1)} %pad_maximum_fusion.6.refs_0_), channel_id=1, source_target_pairs={{0,4},{1,5},{2,6},{3,7},{4,0},{5,1},{6,2},{7,3},{8,12},{9,13},{10,... | collective-permute-start | bytes 1179656 | tf_op jit(solution)/shard_map/ppermute | solution.py:54
  23.1 16.1 %collective-permute-start.8 = (bf16[4,6,16,512]{3,2,1,0:T(8,128)(2,1)S(1)}, bf16[4,6,16,512]{3,2,1,0:T(8,128)(2,1)S(1)}, u32[]{:S(2)}, u32[]{:S(2)}) collective-permute-start(bf16[4,6,16,512]{3,2,1,0:T(8,128)(2,1)S(1)} %pad_maximum_fusion.6.refs_0_), channel_id=1, source_target_pairs={{0,6},{1,7},{2,4},{3,5},{4,2},{5,3},{6,0},{7,1},{8,14},{9,15},{10,... | collective-permute-start | bytes 1179656 | tf_op jit(solution)/shard_map/ppermute | solution.py:54
  23.6 8.6 %collective-permute-start.4 = (bf16[9,16,512]{2,1,0:T(8,128)(2,1)S(1)}, bf16[9,16,512]{2,1,0:T(8,128)(2,1)S(1)}, u32[]{:S(2)}, u32[]{:S(2)}) collective-permute-start(bf16[9,16,512]{2,1,0:T(8,128)(2,1)S(1)} %constant_dynamic-update-slice_fusion), channel_id=1, source_target_pairs={{0,16},{1,17},{2,18},{3,19},{4,20},{5,21},{6,22},{7,23},{8,24},{9,... | collective-permute-start | bytes 442376 | tf_op jit(solution)/shard_map/ppermute | solution.py:54
  25.2 8.8 %collective-permute-start.3 = (bf16[9,16,512]{2,1,0:T(8,128)(2,1)S(1)}, bf16[9,16,512]{2,1,0:T(8,128)(2,1)S(1)}, u32[]{:S(2)}, u32[]{:S(2)}) collective-permute-start(bf16[9,16,512]{2,1,0:T(8,128)(2,1)S(1)} %constant_dynamic-update-slice_fusion), channel_id=1, source_target_pairs={{0,8},{1,9},{2,10},{3,11},{4,12},{5,13},{6,14},{7,15},{8,0},{9,1},... | collective-permute-start | bytes 442376 | tf_op jit(solution)/shard_map/ppermute | solution.py:54
  34.0 6.6 copy-start.52
  34.1 136.6 %copy-start.8 = (bf16[4,9,16,512]{3,2,1,0:T(8,128)(2,1)}, bf16[4,9,16,512]{3,2,1,0:T(8,128)(2,1)S(1)}, u32[]{:S(2)}) copy-start(bf16[4,9,16,512]{3,2,1,0:T(8,128)(2,1)S(1)} %pad_maximum_fusion.5.refs_0_) | copy-start | bytes 1769476
  34.1 7.6 %copy-start.53 = (s32[1024]{0:T(1024)S(1)}, s32[1024]{0:T(1024)}, u32[]{:S(2)}) copy-start(s32[1024]{0:T(1024)} %param.24) | copy-start | bytes 12292
  34.1 8.6 %copy-start = (bf16[1024,512]{1,0:T(8,128)(2,1)S(1)}, bf16[1024,512]{1,0:T(8,128)(2,1)}, u32[]{:S(2)}) copy-start(bf16[1024,512]{1,0:T(8,128)(2,1)} %param.22) | copy-start | bytes 3145732
  34.1 6.5 copy-start.23
  40.6 6.5 collective-permute-start.9
  43.5 127.1 %collective-permute-start.10 = (bf16[4,9,16,512]{3,2,1,0:T(8,128)(2,1)S(1)}, bf16[4,9,16,512]{3,2,1,0:T(8,128)(2,1)S(1)}, u32[]{:S(2)}, u32[]{:S(2)}) collective-permute-start(bf16[4,9,16,512]{3,2,1,0:T(8,128)(2,1)S(1)} %pad_maximum_fusion.5.refs_0_), channel_id=1, source_target_pairs={{0,2},{1,3},{2,0},{3,1},{4,6},{5,7},{6,4},{7,5},{8,10},{9,11},{10,... | collective-permute-start | bytes 1769480 | tf_op jit(solution)/shard_map/ppermute | solution.py:54
  44.7 125.9 %collective-permute-start.11 = (bf16[4,9,16,512]{3,2,1,0:T(8,128)(2,1)S(1)}, bf16[4,9,16,512]{3,2,1,0:T(8,128)(2,1)S(1)}, u32[]{:S(2)}, u32[]{:S(2)}) collective-permute-start(bf16[4,9,16,512]{3,2,1,0:T(8,128)(2,1)S(1)} %pad_maximum_fusion.5.refs_0_), channel_id=1, source_target_pairs={{0,4},{1,5},{2,6},{3,7},{4,0},{5,1},{6,2},{7,3},{8,12},{9,13},{10,... | collective-permute-start | bytes 1769480 | tf_op jit(solution)/shard_map/ppermute | solution.py:54
  45.6 125.1 %collective-permute-start.12 = (bf16[4,9,16,512]{3,2,1,0:T(8,128)(2,1)S(1)}, bf16[4,9,16,512]{3,2,1,0:T(8,128)(2,1)S(1)}, u32[]{:S(2)}, u32[]{:S(2)}) collective-permute-start(bf16[4,9,16,512]{3,2,1,0:T(8,128)(2,1)S(1)} %pad_maximum_fusion.5.refs_0_), channel_id=1, source_target_pairs={{0,6},{1,7},{2,4},{3,5},{4,2},{5,3},{6,0},{7,1},{8,14},{9,15},{10,... | collective-permute-start | bytes 1769480 | tf_op jit(solution)/shard_map/ppermute | solution.py:54
  172.7 7.7 %collective-permute-start.13 = (bf16[16,9,16,512]{3,2,1,0:T(8,128)(2,1)}, bf16[16,9,16,512]{3,2,1,0:T(8,128)(2,1)}, u32[]{:S(2)}, u32[]{:S(2)}) collective-permute-start(bf16[16,9,16,512]{3,2,1,0:T(8,128)(2,1)} %pad_maximum_fusion), channel_id=1, source_target_pairs={{0,1},{1,0},{2,3},{3,2},{4,5},{5,4},{6,7},{7,6},{8,9},{9,8},{10,11... | collective-permute-start | bytes 7077896 | tf_op jit(solution)/shard_map/ppermute | solution.py:54
  340.7 4.7 copy-start.63
  524.0 33.7 %collective-permute-start.14 = (bf16[16,10,16,512]{3,2,1,0:T(8,128)(2,1)}, bf16[16,10,16,512]{3,2,1,0:T(8,128)(2,1)}, u32[]{:S(2)}, u32[]{:S(2)}) collective-permute-start(bf16[16,10,16,512]{3,2,1,0:T(8,128)(2,1)} %get-tuple-element.76), channel_id=1, source_target_pairs={{0,1},{1,0},{2,3},{3,2},{4,5},{5,4},{6,7},{7,6},{8,9},{9,8},{10,11... | collective-permute-start | bytes 7864328 | tf_op jit(solution)/shard_map/ppermute | solution.py:54
  554.4 3.3 copy-start.38
  554.4 3.3 copy-start.39
  571.2 9.7 %copy-start.15 = (bf16[1024,512]{1,0:T(8,128)(2,1)S(1)}, bf16[1024,512]{1,0:T(8,128)(2,1)}, u32[]{:S(2)}) copy-start(bf16[1024,512]{1,0:T(8,128)(2,1)} %copy-done.14) | copy-start | bytes 3145732
  576.5 88.0 %collective-permute-start.15 = (bf16[4,10,16,512]{3,2,1,0:T(8,128)(2,1)}, bf16[4,10,16,512]{3,2,1,0:T(8,128)(2,1)}, u32[]{:S(2)}, u32[]{:S(2)}) collective-permute-start(bf16[4,10,16,512]{3,2,1,0:T(8,128)(2,1)} %get-tuple-element.135), channel_id=1, source_target_pairs={{0,2},{1,3},{2,0},{3,1},{4,6},{5,7},{6,4},{7,5},{8,10},{9,11},{10,... | collective-permute-start | bytes 1966088 | tf_op jit(solution)/shard_map/ppermute | solution.py:54
  577.7 86.8 %collective-permute-start.16 = (bf16[4,10,16,512]{3,2,1,0:T(8,128)(2,1)}, bf16[4,10,16,512]{3,2,1,0:T(8,128)(2,1)}, u32[]{:S(2)}, u32[]{:S(2)}) collective-permute-start(bf16[4,10,16,512]{3,2,1,0:T(8,128)(2,1)} %get-tuple-element.134), channel_id=1, source_target_pairs={{0,4},{1,5},{2,6},{3,7},{4,0},{5,1},{6,2},{7,3},{8,12},{9,13},{10,... | collective-permute-start | bytes 1966088 | tf_op jit(solution)/shard_map/ppermute | solution.py:54
  578.5 86.0 %collective-permute-start.17 = (bf16[4,10,16,512]{3,2,1,0:T(8,128)(2,1)}, bf16[4,10,16,512]{3,2,1,0:T(8,128)(2,1)}, u32[]{:S(2)}, u32[]{:S(2)}) collective-permute-start(bf16[4,10,16,512]{3,2,1,0:T(8,128)(2,1)} %get-tuple-element.133), channel_id=1, source_target_pairs={{0,6},{1,7},{2,4},{3,5},{4,2},{5,3},{6,0},{7,1},{8,14},{9,15},{10,... | collective-permute-start | bytes 1966088 | tf_op jit(solution)/shard_map/ppermute | solution.py:54
  664.5 6.7 copy-start.26
  664.5 6.6 collective-permute-start.21
  666.7 9.1 %collective-permute-start.20 = (bf16[10,16,512]{2,1,0:T(8,128)(2,1)S(1)}, bf16[10,16,512]{2,1,0:T(8,128)(2,1)S(1)}, u32[]{:S(2)}, u32[]{:S(2)}) collective-permute-start(bf16[10,16,512]{2,1,0:T(8,128)(2,1)S(1)} %get-tuple-element.138), channel_id=1, source_target_pairs={{0,24},{1,25},{2,26},{3,27},{4,28},{5,29},{6,30},{7,31},{8,16},{9,... | collective-permute-start | bytes 491528 | tf_op jit(solution)/shard_map/ppermute | solution.py:54
  668.5 13.6 %collective-permute-start.19 = (bf16[10,16,512]{2,1,0:T(8,128)(2,1)S(1)}, bf16[10,16,512]{2,1,0:T(8,128)(2,1)S(1)}, u32[]{:S(2)}, u32[]{:S(2)}) collective-permute-start(bf16[10,16,512]{2,1,0:T(8,128)(2,1)S(1)} %get-tuple-element.139), channel_id=1, source_target_pairs={{0,16},{1,17},{2,18},{3,19},{4,20},{5,21},{6,22},{7,23},{8,24},{9,... | collective-permute-start | bytes 491528 | tf_op jit(solution)/shard_map/ppermute | solution.py:54
  668.5 8.5 %copy-start.2 = (f32[1024,512]{1,0:T(8,128)S(1)}, f32[1024,512]{1,0:T(8,128)}, u32[]{:S(2)}) copy-start(f32[1024,512]{1,0:T(8,128)} %copy-done.1) | copy-start | bytes 6291460
  668.5 8.5 %copy-start.5 = (f32[1024,512]{1,0:T(8,128)S(1)}, f32[1024,512]{1,0:T(8,128)}, u32[]{:S(2)}) copy-start(f32[1024,512]{1,0:T(8,128)} %get-tuple-element.180) | copy-start | bytes 6291460
  668.5 13.6 %collective-permute-start.18 = (bf16[10,16,512]{2,1,0:T(8,128)(2,1)S(1)}, bf16[10,16,512]{2,1,0:T(8,128)(2,1)S(1)}, u32[]{:S(2)}, u32[]{:S(2)}) collective-permute-start(bf16[10,16,512]{2,1,0:T(8,128)(2,1)S(1)} %get-tuple-element.137), channel_id=1, source_target_pairs={{0,8},{1,9},{2,10},{3,11},{4,12},{5,13},{6,14},{7,15},{8,0},{9,1},... | collective-permute-start | bytes 491528 | tf_op jit(solution)/shard_map/ppermute | solution.py:54
  671.7 12.5 %collective-permute-start.24 = (bf16[4,5,16,512]{3,2,1,0:T(8,128)(2,1)S(1)}, bf16[4,5,16,512]{3,2,1,0:T(8,128)(2,1)S(1)}, u32[]{:S(2)}, u32[]{:S(2)}) collective-permute-start(bf16[4,5,16,512]{3,2,1,0:T(8,128)(2,1)S(1)} %get-tuple-element.142), channel_id=1, source_target_pairs={{0,6},{1,7},{2,4},{3,5},{4,2},{5,3},{6,0},{7,1},{8,14},{9,15},{10,... | collective-permute-start | bytes 983048 | tf_op jit(solution)/shard_map/ppermute | solution.py:54
  673.2 15.6 %collective-permute-start.23 = (bf16[4,5,16,512]{3,2,1,0:T(8,128)(2,1)S(1)}, bf16[4,5,16,512]{3,2,1,0:T(8,128)(2,1)S(1)}, u32[]{:S(2)}, u32[]{:S(2)}) collective-permute-start(bf16[4,5,16,512]{3,2,1,0:T(8,128)(2,1)S(1)} %get-tuple-element.143), channel_id=1, source_target_pairs={{0,4},{1,5},{2,6},{3,7},{4,0},{5,1},{6,2},{7,3},{8,12},{9,13},{10,... | collective-permute-start | bytes 983048 | tf_op jit(solution)/shard_map/ppermute | solution.py:54
  675.7 13.2 %collective-permute-start.22 = (bf16[4,5,16,512]{3,2,1,0:T(8,128)(2,1)S(1)}, bf16[4,5,16,512]{3,2,1,0:T(8,128)(2,1)S(1)}, u32[]{:S(2)}, u32[]{:S(2)}) collective-permute-start(bf16[4,5,16,512]{3,2,1,0:T(8,128)(2,1)S(1)} %get-tuple-element.141), channel_id=1, source_target_pairs={{0,2},{1,3},{2,0},{3,1},{4,6},{5,7},{6,4},{7,5},{8,10},{9,11},{10,... | collective-permute-start | bytes 983048 | tf_op jit(solution)/shard_map/ppermute | solution.py:54
  684.1 37.8 %copy-start.60 = (f32[64]{0:T(128)S(1)}, f32[64]{0:T(128)}, u32[]{:S(2)}) copy-start(f32[64]{0:T(128)} %param.41) | copy-start | bytes 772
  684.1 37.8 %copy-start.61 = (f32[64]{0:T(128)S(1)}, f32[64]{0:T(128)}, u32[]{:S(2)}) copy-start(f32[64]{0:T(128)} %param.42) | copy-start | bytes 772
  684.1 37.8 %copy-start.62 = (f32[64]{0:T(128)S(1)}, f32[64]{0:T(128)}, u32[]{:S(2)}) copy-start(f32[64]{0:T(128)} %param.43) | copy-start | bytes 772
  684.1 38.4 %copy-start.31 = (f32[64,512]{1,0:T(8,128)S(1)}, f32[64,512]{1,0:T(8,128)}, u32[]{:S(2)}) copy-start(f32[64,512]{1,0:T(8,128)} %param.35) | copy-start | bytes 393220
  684.1 38.4 %copy-start.44 = (f32[64,512]{1,0:T(8,128)S(1)}, f32[64,512]{1,0:T(8,128)}, u32[]{:S(2)}) copy-start(f32[64,512]{1,0:T(8,128)} %param.36) | copy-start | bytes 393220
  684.1 38.4 %copy-start.45 = (f32[64,512]{1,0:T(8,128)S(1)}, f32[64,512]{1,0:T(8,128)}, u32[]{:S(2)}) copy-start(f32[64,512]{1,0:T(8,128)} %param.37) | copy-start | bytes 393220
  688.9 34.4 %copy-start.57 = (f32[7,16]{1,0:T(8,128)S(1)}, f32[7,16]{1,0:T(8,128)}, u32[]{:S(2)}) copy-start(f32[7,16]{1,0:T(8,128)} %param.38) | copy-start | bytes 1348
  688.9 34.4 %copy-start.58 = (f32[7,16]{1,0:T(8,128)S(1)}, f32[7,16]{1,0:T(8,128)}, u32[]{:S(2)}) copy-start(f32[7,16]{1,0:T(8,128)} %param.39) | copy-start | bytes 1348
  688.9 34.4 %copy-start.59 = (f32[7,16]{1,0:T(8,128)S(1)}, f32[7,16]{1,0:T(8,128)}, u32[]{:S(2)}) copy-start(f32[7,16]{1,0:T(8,128)} %param.40) | copy-start | bytes 1348
  688.9 35.0 %copy-start.32 = (f32[4,16,512]{2,1,0:T(8,128)S(1)}, f32[4,16,512]{2,1,0:T(8,128)}, u32[]{:S(2)}) copy-start(f32[4,16,512]{2,1,0:T(8,128)} %param.26) | copy-start | bytes 393220
  688.9 35.0 %copy-start.46 = (f32[4,16,512]{2,1,0:T(8,128)S(1)}, f32[4,16,512]{2,1,0:T(8,128)}, u32[]{:S(2)}) copy-start(f32[4,16,512]{2,1,0:T(8,128)} %param.27) | copy-start | bytes 393220
  688.9 35.0 %copy-start.47 = (f32[4,16,512]{2,1,0:T(8,128)S(1)}, f32[4,16,512]{2,1,0:T(8,128)}, u32[]{:S(2)}) copy-start(f32[4,16,512]{2,1,0:T(8,128)} %param.28) | copy-start | bytes 393220
  689.1 35.6 %copy-start.43 = (f32[2,16,512]{2,1,0:T(8,128)S(1)}, f32[2,16,512]{2,1,0:T(8,128)}, u32[]{:S(2)}) copy-start(f32[2,16,512]{2,1,0:T(8,128)} %param.29) | copy-start | bytes 196612
  689.1 35.6 %copy-start.50 = (f32[2,16,512]{2,1,0:T(8,128)S(1)}, f32[2,16,512]{2,1,0:T(8,128)}, u32[]{:S(2)}) copy-start(f32[2,16,512]{2,1,0:T(8,128)} %param.30) | copy-start | bytes 196612
  689.1 35.6 %copy-start.51 = (f32[2,16,512]{2,1,0:T(8,128)S(1)}, f32[2,16,512]{2,1,0:T(8,128)}, u32[]{:S(2)}) copy-start(f32[2,16,512]{2,1,0:T(8,128)} %param.31) | copy-start | bytes 196612
  689.1 7.2 collective-permute-start.27
  691.0 7.8 %collective-permute-start.26 = (bf16[5,16,512]{2,1,0:T(8,128)(2,1)S(1)}, bf16[5,16,512]{2,1,0:T(8,128)(2,1)S(1)}, u32[]{:S(2)}, u32[]{:S(2)}) collective-permute-start(bf16[5,16,512]{2,1,0:T(8,128)(2,1)S(1)} %get-tuple-element.159), channel_id=1, source_target_pairs={{0,16},{1,17},{2,18},{3,19},{4,20},{5,21},{6,22},{7,23},{8,24},{9,... | collective-permute-start | bytes 245768 | tf_op jit(solution)/shard_map/ppermute | solution.py:54
  691.0 7.8 %collective-permute-start.25 = (bf16[5,16,512]{2,1,0:T(8,128)(2,1)S(1)}, bf16[5,16,512]{2,1,0:T(8,128)(2,1)S(1)}, u32[]{:S(2)}, u32[]{:S(2)}) collective-permute-start(bf16[5,16,512]{2,1,0:T(8,128)(2,1)S(1)} %get-tuple-element.157), channel_id=1, source_target_pairs={{0,8},{1,9},{2,10},{3,11},{4,12},{5,13},{6,14},{7,15},{8,0},{9,1},... | collective-permute-start | bytes 245768 | tf_op jit(solution)/shard_map/ppermute | solution.py:54
  693.6 31.9 %copy-start.33 = (f32[16,2048]{1,0:T(8,128)S(1)}, f32[16,2048]{1,0:T(8,128)}, u32[]{:S(2)}) copy-start(f32[16,2048]{1,0:T(8,128)} %param.32) | copy-start | bytes 393220
  693.6 31.9 %copy-start.48 = (f32[16,2048]{1,0:T(8,128)S(1)}, f32[16,2048]{1,0:T(8,128)}, u32[]{:S(2)}) copy-start(f32[16,2048]{1,0:T(8,128)} %param.33) | copy-start | bytes 393220
  693.6 31.9 %copy-start.49 = (f32[16,2048]{1,0:T(8,128)S(1)}, f32[16,2048]{1,0:T(8,128)}, u32[]{:S(2)}) copy-start(f32[16,2048]{1,0:T(8,128)} %param.34) | copy-start | bytes 393220
  702.1 1.2 collective-permute-start.28
  703.9 3.6 collective-permute-start.29
  708.1 3.6 collective-permute-start.30
  712.3 3.6 collective-permute-start.31
  716.6 4.5 collective-permute-start.32
  (33 other events, 58.9 us)
where the time goes:
time: 733 us; the launch traced here: 728 us
  Pallas kernels  522 us (71%)
  matrix products  54.9 us (7%)
  starting transfers between devices  47.7 us (7%)
  waiting for transfers between devices  37 us (5%)
  other arithmetic  34.8 us (5%)
  local copies, waits for them, and re-layouts  23.6 us (3%)
  between operations  8.13 us (1%)
    pallas_call x2, Pallas kernels, place(): pl.pallas_call(functools.partial(place_kernel, offsets, layout), in_specs...  240 us
    pallas_call x2, Pallas kernels, split(): pl.pallas_call(functools.partial(split_kernel, offsets, layout), in_specs...  240 us
    ppermute x33, starting transfers between devices, swap_with(): lax.ppermute(array, AXES, [(source, source ^ offset) for source in range(...  47.7 us
    ppermute x33, waiting for transfers between devices, swap_with(): lax.ppermute(array, AXES, [(source, source ^ offset) for source in range(...  37 us
    pallas_call x2, Pallas kernels, attend_back(): pl.pallas_call(attn_bwd_kernel, grid=(pairs,), in_specs=[col, col, row, r...  26.2 us
  transfers between devices with their start and end apart: 33, of which 17 were waited for; matrix products, arithmetic and copies ran while one was open for 6% of the time, Pallas kernels for 30%

commit v1 on v0

--- a/solution.py
+++ b/solution.py
@@ -82,24 +82,47 @@
     return table + [[offset | 1 for row in table for offset in row]]
 
 
-def any_spec():
-    return pl.BlockSpec(memory_space=pl.ANY)
+def vmem_spec():
+    return pl.BlockSpec(memory_space=pltpu.VMEM)
+
+
+def smem_spec():
+    return pl.BlockSpec(memory_space=pltpu.SMEM)
+
+
+def matrix_shape(kind, pieces, count, step, width):
+    if kind == "stack":
+        return (pieces, count, step, width)
+    if kind == "rows":
+        return (count, pieces, step, width)
+    return (count, step, pieces * width)
 
 
 def place_kernel(offsets, layout, own_ref, *refs):
     parts = refs[: len(offsets)]
-    outs = refs[len(offsets) : len(offsets) + len(layout)]
-    sems = refs[-1]
+    outs = refs[len(offsets) :]
     own = own_ref[0]
+    total = None
     for part, row in zip(parts, offsets):
         for entry, offset in enumerate(row):
             owner = own ^ offset
-            for index, (first, pieces) in enumerate(layout):
-                pltpu.make_async_copy(
-                    part.at[entry, first : first + pieces], outs[index].at[:, owner], sems.at[index]
-                ).start()
-    for index in range(len(layout)):
-        pltpu.make_async_copy(outs[index], outs[index], sems.at[index]).wait()
+            for index, (kind, first, pieces) in enumerate(layout):
+                width = part.shape[3]
+                if kind == "sum":
+                    block = part[entry, first].astype(jnp.float32)
+                    total = block if total is None else total + block
+                elif kind == "stack":
+                    for piece in range(pieces):
+                        outs[index][piece, owner] = part[entry, first + piece]
+                elif kind == "rows":
+                    for piece in range(pieces):
+                        outs[index][owner, piece] = part[entry, first + piece]
+                else:
+                    for piece in range(pieces):
+                        outs[index][owner, :, piece * width : (piece + 1) * width] = part[entry, first + piece]
+    for index, (kind, _, _) in enumerate(layout):
+        if kind == "sum":
+            outs[index][...] = total
 
 
 def place(own, parts, layout, groups):
@@ -108,52 +131,80 @@
     offsets = offsets_of(groups)
     if step % 16:
         order = jnp.argsort(jnp.array([o for row in offsets for o in row]) ^ own)
-        full = jnp.moveaxis(jnp.concatenate(parts)[order], 0, 1)
-        return [full[first : first + pieces] for first, pieces in layout]
+        full = jnp.concatenate(parts)[order]
+        result = []
+        for kind, first, pieces in layout:
+            chosen = full[:, first : first + pieces]
+            if kind == "sum":
+                result.append(jnp.sum(chosen.astype(jnp.float32), 0).reshape(pieces * step, width))
+            elif kind == "stack":
+                result.append(jnp.moveaxis(chosen, 0, 1))
+            elif kind == "rows":
+                result.append(chosen)
+            else:
+                result.append(jnp.moveaxis(chosen, 1, 2).reshape(count, step, pieces * width))
+        return result
+    shapes = [
+        jax.ShapeDtypeStruct((step, width), jnp.float32)
+        if kind == "sum"
+        else jax.ShapeDtypeStruct(matrix_shape(kind, pieces, count, step, width), jnp.bfloat16)
+        for kind, _, pieces in layout
+    ]
     return pl.pallas_call(
         functools.partial(place_kernel, offsets, layout),
-        in_specs=[pl.BlockSpec(memory_space=pltpu.SMEM)] + [any_spec() for _ in parts],
-        out_specs=[any_spec() for _ in layout],
-        out_shape=[jax.ShapeDtypeStruct((pieces, count, step, width), jnp.bfloat16) for _, pieces in layout],
-        scratch_shapes=[pltpu.SemaphoreType.DMA((len(layout),))],
+        in_specs=[smem_spec()] + [vmem_spec() for _ in parts],
+        out_specs=[vmem_spec() for _ in layout],
+        out_shape=shapes,
         name="place",
     )(own[None].astype(jnp.int32), *parts)
 
 
 def split_kernel(offsets, layout, own_ref, *refs):
     ins = refs[: len(layout)]
-    kept, sent, sems = refs[len(layout) :]
+    kept, sent = refs[len(layout) :]
     own = own_ref[0]
     for entry, offset in enumerate(offsets):
         for side, target in enumerate((kept, sent)):
             owner = own ^ (offset | side)
-            for index, (first, pieces) in enumerate(layout):
-                pltpu.make_async_copy(
-                    ins[index].at[:, owner], target.at[entry, first : first + pieces], sems.at[side]
-                ).start()
-    pltpu.make_async_copy(kept, kept, sems.at[0]).wait()
-    pltpu.make_async_copy(sent, sent, sems.at[1]).wait()
-
-
-def split(own, grads, groups):
-    step, width = grads[0].shape[2:]
-    layout = []
-    first = 0
-    for grad in grads:
-        layout.append((first, grad.shape[0]))
-        first += grad.shape[0]
+            for index, (kind, first, pieces) in enumerate(layout):
+                width = target.shape[3]
+                for piece in range(pieces):
+                    if kind == "sum":
+                        block = ins[index][...]
+                    elif kind == "stack":
+                        block = ins[index][piece, owner]
+                    elif kind == "rows":
+                        block = ins[index][owner, piece]
+                    else:
+                        block = ins[index][owner, :, piece * width : (piece + 1) * width]
+                    target[entry, first + piece] = block
+
+
+def split(own, grads, layout, groups):
+    count = 2 ** sum(groups)
+    width = 512
+    total = sum(pieces for _, _, pieces in layout)
+    step = grads[0].shape[-2]
     offsets = [offset for row in offsets_of(groups)[:-1] for offset in row]
     if step % 16:
-        full = jnp.moveaxis(jnp.concatenate(grads), 1, 0)
+        pieces_of = []
+        for grad, (kind, _, pieces) in zip(grads, layout):
+            if kind == "sum":
+                grad = jnp.broadcast_to(grad.reshape(1, pieces, step, width), (count, pieces, step, width))
+            elif kind == "stack":
+                grad = jnp.moveaxis(grad, 1, 0)
+            elif kind == "columns":
+                grad = jnp.moveaxis(grad.reshape(count, step, pieces, width), 2, 1)
+            pieces_of.append(grad)
+        full = jnp.concatenate(pieces_of, 1)
         order = jnp.array(offsets) ^ own
         return full[order], full[order ^ 1]
-    shape = jax.ShapeDtypeStruct((len(offsets), first, step, width), jnp.bfloat16)
+    shape = jax.ShapeDtypeStruct((len(offsets), total, step, width), jnp.bfloat16)
     return pl.pallas_call(
         functools.partial(split_kernel, offsets, layout),
-        in_specs=[pl.BlockSpec(memory_space=pltpu.SMEM)] + [any_spec() for _ in grads],
-        out_specs=[any_spec(), any_spec()],
+        in_specs=[smem_spec()] + [vmem_spec() for _ in grads],
+        out_specs=[vmem_spec(), vmem_spec()],
         out_shape=[shape, shape],
-        scratch_shapes=[pltpu.SemaphoreType.DMA((2,))],
         name="split",
     )(own[None].astype(jnp.int32), *grads)
 
@@ -194,18 +245,22 @@
     return lax.optimization_barrier(values)
 
 
-def small_rows(vec, bias, count, width):
-    step = vec.shape[1] // count
-    rows = jnp.concatenate(
-        [vec.reshape(7, count, step).transpose(1, 0, 2).reshape(count, 7 * step), bias.reshape(count, 4 * step)], 1
-    ).astype(jnp.bfloat16)
-    return jnp.pad(rows, ((0, 0), (0, width - rows.shape[1])))
-
-
-def small_back(rows, step):
-    count = rows.shape[0]
-    vec = rows[:, : 7 * step].reshape(count, 7, step).transpose(1, 0, 2).reshape(7, count * step)
-    return vec, rows[:, 7 * step : 11 * step].reshape(-1)
+def small_shard(vec, bias, own, count, width):
+    step = vec.shape[1]
+    lane = lax.broadcasted_iota(jnp.int32, (7, width), 1)
+    rows = jnp.where(lane // step == own, jnp.tile(vec, (1, count)), 0.0)
+    place_of = lax.broadcasted_iota(jnp.int32, (4, width), 0) * width + lax.broadcasted_iota(
+        jnp.int32, (4, width), 1
+    )
+    tiled = jnp.tile(bias, width // bias.shape[0])[None]
+    bias_rows = jnp.where(place_of // bias.shape[0] == own, tiled, 0.0)
+    return jnp.concatenate([rows, bias_rows])
+
+
+def pad_rows(rows, step):
+    pieces = -(-rows.shape[0] // step)
+    rows = jnp.pad(rows.astype(jnp.bfloat16), ((0, pieces * step - rows.shape[0]), (0, 0)))
+    return rows.reshape(pieces, step, rows.shape[1])
 
 
 def mat(a,b,dims):
@@ -355,9 +410,10 @@
     low = lambda value: value.astype(jnp.bfloat16)
     dot = functools.partial(jnp.einsum, preferred_element_type=jnp.float32)
     columns = lambda value: [value[:, width * j : width * (j + 1)] for j in range(4)]
-    small = jnp.pad(small_rows(norm_params, in_bias, 1, width), ((0, step - 1), (0, 0)))
-    first_shard = jnp.stack(
-        [low(attn_weight[0]), low(attn_weight[1]), low(attn_weight[2]), low(gate_weight[0]), low(attn_weight[3]), small]
+    small = pad_rows(small_shard(norm_params, in_bias, own, count, width), step)
+    extra = small.shape[0]
+    first_shard = jnp.concatenate(
+        [low(attn_weight[:3]), low(gate_weight[:1]), low(attn_weight[3:]), small]
     )
     second_shard = jnp.concatenate(
         [
@@ -372,12 +428,15 @@
     z_second, *plane_first = tie(z_second, *plane_first)
     core_first = gather_core(z_first, plane_first, groups)
     plane_second = gather_plane(z_second, groups)
-    w_four, w_o, small_all = place(
-        own, [z_first] + plane_first + [core_first], [(0, 4), (4, 1), (5, 1)], groups
+    w_four, w_o, vectors = place(
+        own,
+        [z_first] + plane_first + [core_first],
+        [("stack", 0, 4), ("stack", 4, 1), ("sum", 5, extra)],
+        groups,
     )
     w_four = w_four.reshape(4, count * step, width)
     w_o = w_o.reshape(count * step, width)
-    vectors, bias = small_back(small_all[0, :, 0].astype(jnp.float32), step)
+    bias = vectors[7:11].reshape(-1)
     inputs = tokens.astype(jnp.float32)
     normed_full, unit_one, scale_one = normalize_parts(inputs, vectors[0], vectors[1])
     normed = low(normed_full)
@@ -391,11 +450,14 @@
     normed_two_full, unit_two, scale_two = normalize_parts(middle, vectors[2], vectors[3])
     normed_two = low(normed_two_full)
     w_f, w_in, w_out = place(
-        own, [z_second] + plane_second + [core_second], [(0, 1), (1, 4), (5, 4)], groups
+        own,
+        [z_second] + plane_second + [core_second],
+        [("stack", 0, 1), ("columns", 1, 4), ("rows", 5, 4)],
+        groups,
     )
     w_f = w_f.reshape(count * step, width)
-    w_in = jnp.concatenate(list(w_in.reshape(4, count * step, width)), 1)
-    w_out = w_out.transpose(1, 0, 2, 3).reshape(4 * count * step, width)
+    w_in = w_in.reshape(count * step, 4 * width)
+    w_out = w_out.reshape(4 * count * step, width)
     hidden = dot("td,df->tf", normed_two, w_in) + bias
     active = low(jnp.maximum(hidden, 0.0))
     branch = dot("tf,fd->td", active, w_out) + vectors[6]
@@ -423,27 +485,29 @@
     attended_low = low(grad_attended)
     grad_w_o = low(dot("td,te->de", mixed_heads, attended_low))
     grad_mixed = low(dot("te,de->td", attended_low, w_o))
-    blocks = lambda value: value.reshape(-1, count, step, width)
+    blocks = lambda value: value.reshape(1, count, step, width)
     kept_b, sent_b = split(
         own,
         [
             blocks(grad_w_f),
-            blocks(jnp.stack(columns(grad_w_in))),
-            grad_w_out.reshape(count, 4, step, width).transpose(1, 0, 2, 3),
+            grad_w_in.reshape(count, step, 4 * width),
+            grad_w_out.reshape(count, 4, step, width),
             blocks(grad_w_o),
         ],
+        [("stack", 0, 1), ("columns", 1, 4), ("rows", 5, 4), ("stack", 9, 1)],
         groups,
     )
     core_b = swap_with(sent_b, 1, count)
     half_one = attend_back(queries, keys, values, grad_mixed, log_total, segments, positions, 0, 2)
     core_b, kept_b, *half_one = tie(core_b, kept_b, *half_one)
     own_b, plane_b = reduce_plane(kept_b, core_b, groups)
+    own_b, log_total = tie(own_b, log_total)
     half_two = attend_back(queries, keys, values, grad_mixed, log_total, segments, positions, 2, 2)
     triple_grad = [jnp.concatenate([one, two], 1) for one, two in zip(half_one, half_two)]
     agate_low = low(grad_agate)
     back_four = triple_grad + [agate_low]
     grad_normed = sum(dot("te,de->td", back_four[j], w_four[j]) for j in range(4))
-    grad_w_four = jnp.stack([low(dot("td,te->de", normed, back_four[j])) for j in range(4)])
+    grad_w_four = [low(dot("td,te->de", normed, back_four[j])) for j in range(4)]
     grad_gain_one = jnp.sum(grad_normed * unit_one, 0)
     grad_shift_one = jnp.sum(grad_normed, 0)
     grad_inputs = grad_inputs + normalize_back(grad_normed, unit_one, scale_one, vectors[0])
@@ -460,8 +524,13 @@
         ]
     )
     grad_bias = jnp.sum(grad_hidden, 0)
-    grad_small = jnp.pad(small_rows(grad_vectors, grad_bias, count, width)[:, None], ((0, 0), (0, step - 1), (0, 0)))
-    kept_a, sent_a = split(own, [blocks(grad_w_four), grad_small[None]], groups)
+    grad_small = pad_rows(jnp.concatenate([grad_vectors, grad_bias.reshape(4, width)]), step)
+    kept_a, sent_a = split(
+        own,
+        [blocks(grad) for grad in grad_w_four] + [grad_small.reshape(-1, width) if extra == 1 else grad_small],
+        [("stack", j, 1) for j in range(4)] + [("sum", 4, extra)],
+        groups,
+    )
     kept_a, sent_a, *plane_b = tie(kept_a, sent_a, *plane_b)
     core_a = swap_with(sent_a, 1, count)
     own_b, z_b = reduce_z(own_b, plane_b, groups)
@@ -469,8 +538,9 @@
     own_a, z_a = reduce_z(own_a, plane_a, groups)
     total_b = reduce_end(own_b, z_b)
     total_a = reduce_end(own_a, z_a)
-    own_small = total_a[4, :1]
-    own_vec, own_bias = small_back(own_small, step)
+    own_small = total_a[4:].reshape(extra * step, width)
+    own_vec = lax.dynamic_slice(own_small[:7], (0, own * step), (7, step))
+    own_bias = lax.dynamic_slice(own_small[7:11].reshape(-1), (own * 4 * step,), (4 * step,))
     owned = (
         jnp.concatenate([total_a[:3], total_b[9:]]),
         jnp.stack([total_a[3], total_b[0]]),
@@ -479,7 +549,7 @@
         own_vec,
         own_bias,
     )
-    local_squares = jnp.sum(total_b * total_b) + jnp.sum(total_a[:4] * total_a[:4]) + jnp.sum(own_small * own_small)
+    local_squares = jnp.sum(total_b * total_b) + jnp.sum(total_a[:4] * total_a[:4]) + jnp.sum(own_vec * own_vec) + jnp.sum(own_bias * own_bias)
     grad_norm = jnp.sqrt(sum_all(local_squares, groups))
     factor = jnp.minimum(1.0, clip_norm / (grad_norm + 1e-06))
     states = (

time: 733 us -> 267 us (0.36)
  Pallas kernels: 522 us -> 57.6 us
  waiting for transfers between devices: 37 us -> 52.9 us
  local copies, waits for them, and re-layouts: 23.6 us -> 14.9 us
    pallas_call x2, Pallas kernels: 240 us -> 8.3 us  [split(): pl.pallas_call(functools.partial(split_kernel, offsets, layout), in_specs...]
    pallas_call x2, Pallas kernels: 240 us -> 8.48 us  [place(): pl.pallas_call(functools.partial(place_kernel, offsets, layout), in_specs...]
    ppermute x33, waiting for transfers between devices: 37 us -> 52.9 us  [swap_with(): lax.ppermute(array, AXES, [(source, source ^ offset) for source in range(...]
  transfers between devices with their start and end apart: 33 -> 33, of which waited for: 17 -> 15; matrix products, arithmetic and copies ran while one was open for 6% -> 16% of each run, Pallas kernels for 30% -> 13%
where the time goes in v1:
time: 267 us; the launch traced here: 262 us
  Pallas kernels  57.6 us (22%)
  waiting for transfers between devices  52.9 us (20%)
  matrix products  52.8 us (20%)
  starting transfers between devices  45.1 us (17%)
  other arithmetic  30 us (11%)
  local copies, waits for them, and re-layouts  14.9 us (6%)
  between operations  8.78 us (3%)
    ppermute x33, waiting for transfers between devices, swap_with(): lax.ppermute(array, AXES, [(source, source ^ offset) for source in range(...  52.9 us
    ppermute x33, starting transfers between devices, swap_with(): lax.ppermute(array, AXES, [(source, source ^ offset) for source in range(...  45.1 us
    pallas_call x2, Pallas kernels, attend_back(): pl.pallas_call(attn_bwd_kernel, grid=(pairs,), in_specs=[col, col, row, r...  26.1 us
    pallas_call x1, Pallas kernels, attend(): pl.pallas_call(attn_fwd_kernel, grid=(pairs,), in_specs=[col, col, row, r...  14.7 us
    dot_general x4, matrix products, body(): dot('td,te->de', normed, back_four[j])  10.4 us
    pallas_call x2, Pallas kernels, place(): pl.pallas_call(functools.partial(place_kernel, offsets, layout), in_specs...  8.48 us
    pallas_call x2, Pallas kernels, split(): pl.pallas_call(functools.partial(split_kernel, offsets, layout), in_specs...  8.3 us
    unnamed x140, local copies, waits for them, and re-layouts  6.48 us
  transfers between devices with their start and end apart: 33, of which 15 were waited for; matrix products, arithmetic and copies ran while one was open for 16% of the time, Pallas kernels for 13%

profile of v1, /device:TPU:0, one launch (start us, length us, event | category | flops | bytes accessed | tf_op | source)
XLA Modules:
  0.0 262.1 jit_solution(18159489854501474905)
XLA Ops:
  4.2 3.1 %collective-permute-start = (bf16[6,16,512]{2,1,0:T(8,128)(2,1)S(1)}, bf16[6,16,512]{2,1,0:T(8,128)(2,1)S(1)}, u32[]{:S(2)}, u32[]{:S(2)}) collective-permute-start(bf16[6,16,512]{2,1,0:T(8,128)(2,1)S(1)} %get-tuple-element.163), channel_id=1, source_target_pairs={{0,8},{1,9},{2,10},{3,11},{4,12},{5,13},{6,14},{7,15},{8,0},{9,1},... | collective-permute-start | bytes 294920 | tf_op jit(solution)/shard_map/ppermute | solution.py:54
  7.3 2.6 collective-permute-start.1
  11.8 5.9 %collective-permute-done.1 = bf16[6,16,512]{2,1,0:T(8,128)(2,1)S(1)} collective-permute-done((bf16[6,16,512]{2,1,0:T(8,128)(2,1)S(1)}, bf16[6,16,512]{2,1,0:T(8,128)(2,1)S(1)}, u32[]{:S(2)}, u32[]{:S(2)}) %collective-permute-start.1) | collective-permute-done | bytes 98336 | tf_op jit(solution)/shard_map/ppermute | solution.py:54
  17.8 1.7 collective-permute-start.3
  19.5 1.5 collective-permute-start.6
  21.0 1.5 collective-permute-start.7
  23.0 1.4 collective-permute-start.4
  24.4 1.4 collective-permute-start.5
  25.8 8.8 %collective-permute-done.4 = bf16[9,16,512]{2,1,0:T(8,128)(2,1)S(1)} collective-permute-done((bf16[9,16,512]{2,1,0:T(8,128)(2,1)S(1)}, bf16[9,16,512]{2,1,0:T(8,128)(2,1)S(1)}, u32[]{:S(2)}, u32[]{:S(2)}) %collective-permute-start.4) | collective-permute-done | bytes 147488 | tf_op jit(solution)/shard_map/ppermute | solution.py:54
  34.8 3.8 %collective-permute-done.7.refs_2_ = bf16[4,6,16,512]{3,2,1,0:T(8,128)(2,1)S(1)} collective-permute-done((bf16[4,6,16,512]{3,2,1,0:T(8,128)(2,1)S(1)}, bf16[4,6,16,512]{3,2,1,0:T(8,128)(2,1)S(1)}, u32[]{:S(2)}, u32[]{:S(2)}) %collective-permute-start.7) | collective-permute-done | bytes 393248 | tf_op jit(solution)/shard_map/ppermute | solution.py:54
  38.6 1.4 pad_maximum_fusion.1
  45.0 1.4 collective-permute-start.12
  46.4 3.6 %place.2 = (bf16[4,32,16,512]{3,2,1,0:T(8,128)(2,1)}, bf16[1,32,16,512]{3,2,1,0:T(8,128)(2,1)}, f32[16,512]{1,0:T(8,128)}) custom-call(s32[1]{0:T(128)} %bitcast.own_ref, bf16[4,6,16,512]{3,2,1,0:T(8,128)(2,1)} %copy-done.10, bf16[4,6,16,512]{3,2,1,0:T(8,128)(2,1)} %copy-done.26, bf16[4,6,16,512]{3,2,1,0:T(8,128)(2,1)} %copy-done.27, ...), custom_call_target="tpu_custom_call" | custom-call | tf_op jit(solution)/shard_map/place/pallas_call | solution.py:153
  50.0 2.5 fusion.95
  52.6 1.8 convolution_convert_fusion.3.v_ref
  54.4 1.8 convolution_convert_fusion.4.k_ref
  56.2 1.8 convolution_convert_fusion.5.q_ref
  57.9 14.7 %attn_fwd.1 = (bf16[1024,512]{1,0:T(8,128)(2,1)}, f32[4,2,1024]{2,1,0:T(2,128)}) custom-call(s32[1024,1]{1,0:T(8,128)} %copy.43.segc, s32[1024,1]{1,0:T(8,128)} %copy.44.posc, s32[1,1024]{1,0:T(1,128)} %bitcast.167, s32[1,1024]{1,0:T(1,128)} %bitcast.171, bf16[1024,512]{1,0:T(8,128)(2,1)} %convolution_convert_fusion.5.q_ref, ...), custom_call_target="tpu_custom_call" | custom-call | tf_op jit(solution)/shard_map/attn_fwd/pallas_call | solution.py:346
  75.3 1.4 fusion.93
  77.2 1.4 add_convert_fusion.1
  78.6 4.9 %place.3 = (bf16[1,32,16,512]{3,2,1,0:T(8,128)(2,1)}, bf16[32,16,2048]{2,1,0:T(8,128)(2,1)}, bf16[32,4,16,512]{3,2,1,0:T(8,128)(2,1)}) custom-call(s32[1]{0:T(128)} %bitcast.own_ref, bf16[4,9,16,512]{3,2,1,0:T(8,128)(2,1)} %copy-done.8, bf16[4,9,16,512]{3,2,1,0:T(8,128)(2,1)} %copy-done.12, bf16[4,9,16,512]{3,2,1,0:T(8,128)(2,1)} %copy-done.13, ...), custom_call_target="tpu_custom_call" | custom-call | tf_op jit(solution)/shard_map/place/pallas_call | solution.py:153
  83.5 4.4 %fusion.99 = f32[1024,2048]{1,0:T(8,128)S(1)} fusion(bf16[1024,512]{1,0:T(8,128)(2,1)} %add_convert_fusion.1, bf16[512,2048]{1,0:T(8,128)(2,1)} %bitcast.205), kind=kOutput, calls=%fused_computation.200 | convolution fusion | flops 2147483648 | bytes 11534336 | tf_op jit(solution)/shard_map/td,df->tf/dot_general | solution.py:461
  89.1 3.7 %convolution_convert_fusion = bf16[2048,512]{1,0:T(8,128)(2,1)} fusion(f32[1024,2048]{1,0:T(8,128)S(1)} %fusion.99, f32[2048]{0:T(1024)S(1)} %bitcast.191, f32[1024,512]{1,0:T(8,128)S(1)} %add_divide_fusion, bf16[1024,512]{1,0:T(8,128)(2,1)S(1)} %copy-done.30), kind=kOutput, calls=%fused_computation.9 | convolution fusion | flops 2156396544 | bytes 13639680 | tf_op jit(solution)/shard_map/tf,td->fd/dot_general | solution.py:471
  92.8 2.9 %fusion.97 = (bf16[2048]{0:T(1024)(128)(2,1)S(1)}, bf16[1024,2048]{1,0:T(8,128)(2,1)S(1)}) fusion(bf16[2048,512]{1,0:T(8,128)(2,1)S(1)} %bitcast.207, f32[1024,512]{1,0:T(8,128)S(1)} %add_divide_fusion, bf16[1024,512]{1,0:T(8,128)(2,1)S(1)} %copy-done.30, f32[1024,2048]{1,0:T(8,128)S(1)} %fusion.99, f32[2048]{0:T(1024)S(1)} %bitcast.192), kind=kOutput, calls=%fused_computation.198 | convolution fusion | flops 2159540224 | bytes 17838080 | tf_op jit(solution)/shard_map/td,fd->tf/dot_general | solution.py:472
  95.8 4.0 %fusion.88 = (bf16[512]{0:T(512)(128)(2,1)S(1)}, bf16[1024,512]{1,0:T(8,128)(2,1)S(1)}, bf16[1024,512]{1,0:T(8,128)(2,1)}, bf16[512]{0:T(512)(128)(2,1)S(1)}) fusion(f32[1024,512]{1,0:T(8,128)S(1)} %add_divide_fusion, f32[1024,512]{1,0:T(8,128)S(1)} %copy-done.4, f32[512]{0:T(512)S(1)} %bitcast.202, bf16[1024,512]{1,0:T(8,128)(2,1)S(1)} %copy-done.30, ...), kind=kOutput, calls=%fused_computation.193 | convolution fusion | flops 2161638400 | bytes 17838080 | tf_op jit(solution)/shard_map/tf,fd->td/dot_general | solution.py:463
  100.6 1.6 convolution_convert_fusion.11
  102.1 3.7 %convolution_convert_fusion.1 = bf16[512,2048]{1,0:T(8,128)(2,1)} fusion(bf16[1024,512]{1,0:T(8,128)(2,1)S(1)} %copy-done.34, bf16[1024,2048]{1,0:T(8,128)(2,1)S(1)} %get-tuple-element.177), kind=kOutput, calls=%fused_computation.10 | convolution fusion | flops 2148532224 | bytes 7340032 | tf_op jit(solution)/shard_map/td,tf->df/dot_general | solution.py:475
  105.8 3.1 %multiply_reduce_fusion = (bf16[512]{0:T(512)(128)(2,1)S(1)}, f32[1024]{0:T(1024)S(1)}, f32[1024]{0:T(1024)S(1)}, bf16[512]{0:T(512)(128)(2,1)S(1)}, f32[1024,512]{1,0:T(8,128)S(1)}) fusion(f32[1024,512]{1,0:T(8,128)S(1)} %copy-done.4, f32[1024]{0:T(1024)S(1)} %add_rsqrt_fusion, f32[1024]{0:T(1024)S(1)} %broadcast_multiply_fusion.4, f32[512]{0:T(512)S(1)} %bitcast.186, ...), kind=kOutput, calls=%fused_computation.34 | convolution fusion | flops 2152723456 | bytes 12603392 | tf_op jit(solution)/shard_map/tf,df->td/dot_general | solution.py:478
  109.0 2.7 %fusion.90 = (bf16[512]{0:T(512)(128)(2,1)S(1)}, bf16[1024,512]{1,0:T(8,128)(2,1)}, f32[1024,512]{1,0:T(8,128)S(1)}) fusion(f32[1024,512]{1,0:T(8,128)S(1)} %get-tuple-element.173, f32[1024,512]{1,0:T(8,128)S(1)} %copy-done.7, bf16[1024,512]{1,0:T(8,128)(2,1)S(1)} %copy-done, f32[1024]{0:T(1024)S(1)} %broadcast_multiply_fusion.2, ...), kind=kLoop, calls=%fused_computation.194 | loop fusion | flops 9960960 | bytes 15748096 | tf_op jit(solution)/shard_map/reduce_sum | solution.py:521
  113.7 1.6 convolution_convert_fusion.10
  115.2 5.1 %split.2 = (bf16[16,10,16,512]{3,2,1,0:T(8,128)(2,1)}, bf16[16,10,16,512]{3,2,1,0:T(8,128)(2,1)}) custom-call(s32[1]{0:T(128)} %bitcast.own_ref, bf16[1,32,16,512]{3,2,1,0:T(8,128)(2,1)} %bitcast.157, bf16[32,16,2048]{2,1,0:T(8,128)(2,1)} %bitcast.140, bf16[32,4,16,512]{3,2,1,0:T(8,128)(2,1)} %bitcast.139, bf16[1,32,16,512]{3,2,1,0:T(8,128)(2,1)} %bitcast.158), custom_call_target="tpu_custom_call" | custom-call | tf_op jit(solution)/shard_map/split/pallas_call | solution.py:203
  120.4 3.1 %convolution_convert_fusion.2.do_ref = bf16[1024,512]{1,0:T(8,128)(2,1)} fusion(bf16[1024,512]{1,0:T(8,128)(2,1)} %copy-done.33, bf16[512,512]{1,0:T(8,128)(2,1)} %bitcast.149), kind=kOutput, calls=%fused_computation.51 | convolution fusion | flops 537395200 | bytes 2621440 | tf_op jit(solution)/shard_map/te,de->td/dot_general | solution.py:487
  123.5 12.9 %attn_bwd.2 = (bf16[1024,256]{1,0:T(8,128)(2,1)}, bf16[1024,256]{1,0:T(8,128)(2,1)}, bf16[1024,256]{1,0:T(8,128)(2,1)}) custom-call(s32[1024,1]{1,0:T(8,128)} %copy.43.segc, s32[1024,1]{1,0:T(8,128)} %copy.44.posc, s32[1,1024]{1,0:T(1,128)} %bitcast.168, s32[1,1024]{1,0:T(1,128)} %bitcast.172, bf16[1024,512]{1,0:T(8,128)(2,1)} %convolution_convert_fusion.5.q_ref, ...), custom_call_target="tpu_custom_call" | custom-call | tf_op jit(solution)/shard_map/attn_bwd/pallas_call | solution.py:360
  136.4 3.3 %convolution_convert_fusion.6 = bf16[512,512]{1,0:T(8,128)(2,1)} fusion(bf16[1024,512]{1,0:T(8,128)(2,1)} %get-tuple-element.132, bf16[1024,512]{1,0:T(8,128)(2,1)S(1)} %copy-done, f32[512]{0:T(512)S(1)} %bitcast.198, f32[512]{0:T(512)S(1)} %bitcast.179, f32[1024]{0:T(1024)S(1)} %add_rsqrt_fusion.1, f32[1024]{0:T(1024)S(1)} %broadcast_multiply_fusion.5), kind=kOutput, calls=%fused_computation.61 | convolution fusion | flops 540278784 | bytes 2633728 | tf_op jit(solution)/shard_map/td,te->de/dot_general | solution.py:510
  139.8 4.2 %add_convert_fusion.2 = (bf16[4,10,16,512]{3,2,1,0:T(8,128)(2,1)}, bf16[4,10,16,512]{3,2,1,0:T(8,128)(2,1)}, bf16[4,10,16,512]{3,2,1,0:T(8,128)(2,1)}, f32[4,10,16,512]{3,2,1,0:T(8,128)}) fusion(bf16[16,10,16,512]{3,2,1,0:T(8,128)(2,1)} %collective-permute-done.14, bf16[16,10,16,512]{3,2,1,0:T(8,128)(2,1)S(1)} %copy-done.11), kind=kLoop, calls=%fused_computation.57 | loop fusion | flops 4915200 | bytes 8519680 | tf_op jit(solution)/shard_map/convert_element_type | solution.py:220
  144.0 13.2 %attn_bwd.3 = (bf16[1024,256]{1,0:T(8,128)(2,1)}, bf16[1024,256]{1,0:T(8,128)(2,1)}, bf16[1024,256]{1,0:T(8,128)(2,1)}) custom-call(s32[1024,1]{1,0:T(8,128)} %copy.43.segc, s32[1024,1]{1,0:T(8,128)} %copy.44.posc, s32[1,1024]{1,0:T(1,128)} %bitcast.169, s32[1,1024]{1,0:T(1,128)} %bitcast.173, bf16[1024,512]{1,0:T(8,128)(2,1)} %convolution_convert_fusion.5.q_ref, ...), custom_call_target="tpu_custom_call" | custom-call | tf_op jit(solution)/shard_map/attn_bwd/pallas_call | solution.py:360
  165.8 1.4 collective-permute-start.17
  167.2 3.0 %fusion.13 = (bf16[512]{0:T(512)(128)(2,1)S(1)}, f32[1024]{0:T(1024)S(1)}, f32[1024]{0:T(1024)S(1)}, bf16[512]{0:T(512)(128)(2,1)S(1)}, f32[1024,512]{1,0:T(8,128)}) fusion(bf16[1024,512]{1,0:T(8,128)(2,1)S(1)} %copy-done, f32[1024]{0:T(1024)S(1)} %add_rsqrt_fusion.1, f32[1024]{0:T(1024)S(1)} %broadcast_multiply_fusion.5, f32[512]{0:T(512)S(1)} %bitcast.180, ...), kind=kOutput, calls=%fused_computation.25 | convolution fusion | flops 543683584 | bytes 11030528 | tf_op jit(solution)/shard_map/te,de->td/dot_general | solution.py:509
  170.2 2.0 convolution_convert_fusion.7
  173.2 3.2 %convolution_convert_fusion.8 = bf16[512,512]{1,0:T(8,128)(2,1)} fusion(bf16[1024,512]{1,0:T(8,128)(2,1)} %copy-done.15, bf16[1024,512]{1,0:T(8,128)(2,1)S(1)} %copy-done, f32[512]{0:T(512)S(1)} %bitcast.200, f32[512]{0:T(512)S(1)} %bitcast.182, f32[1024]{0:T(1024)S(1)} %add_rsqrt_fusion.1, f32[1024]{0:T(1024)S(1)} %broadcast_multiply_fusion.5), kind=kOutput, calls=%fused_computation.63 | convolution fusion | flops 540278784 | bytes 2633728 | tf_op jit(solution)/shard_map/td,te->de/dot_general | solution.py:510
  176.5 1.9 convolution_convert_fusion.9
  178.4 3.2 %split.3 = (bf16[16,5,16,512]{3,2,1,0:T(8,128)(2,1)}, bf16[16,5,16,512]{3,2,1,0:T(8,128)(2,1)}) custom-call(s32[1]{0:T(128)} %bitcast.own_ref, bf16[1,32,16,512]{3,2,1,0:T(8,128)(2,1)} %bitcast.156, bf16[1,32,16,512]{3,2,1,0:T(8,128)(2,1)} %bitcast.155, bf16[1,32,16,512]{3,2,1,0:T(8,128)(2,1)} %bitcast.152, bf16[1,32,16,512]{3,2,1,0:T(8,128)(2,1)} %bitcast.151, ...), custom_call_target="tpu_custom_call" | custom-call | tf_op jit(solution)/shard_map/split/pallas_call | solution.py:203
  181.6 12.9 %collective-permute-done.16 = bf16[4,10,16,512]{3,2,1,0:T(8,128)(2,1)} collective-permute-done((bf16[4,10,16,512]{3,2,1,0:T(8,128)(2,1)}, bf16[4,10,16,512]{3,2,1,0:T(8,128)(2,1)}, u32[]{:S(2)}, u32[]{:S(2)}) %collective-permute-start.16) | collective-permute-done | bytes 655392 | tf_op jit(solution)/shard_map/ppermute | solution.py:54
  194.5 1.6 collective-permute-done.17
  196.2 2.1 fusion.36
  198.7 2.7 %collective-permute-start.19 = (bf16[10,16,512]{2,1,0:T(8,128)(2,1)S(1)}, bf16[10,16,512]{2,1,0:T(8,128)(2,1)S(1)}, u32[]{:S(2)}, u32[]{:S(2)}) collective-permute-start(bf16[10,16,512]{2,1,0:T(8,128)(2,1)S(1)} %get-tuple-element.143), channel_id=1, source_target_pairs={{0,16},{1,17},{2,18},{3,19},{4,20},{5,21},{6,22},{7,23},{8,24},{9,... | collective-permute-start | bytes 491528 | tf_op jit(solution)/shard_map/ppermute | solution.py:54
  201.4 1.4 collective-permute-start.20
  202.7 1.8 add_convert_fusion.7
  205.4 1.5 collective-permute-start.23
  208.0 1.7 collective-permute-start.24
  209.7 1.9 fusion.12
  211.6 2.1 collective-permute-done.19
  213.7 2.0 multiply_reduce_fusion.5
  215.8 5.8 %collective-permute-done.23 = bf16[4,5,16,512]{3,2,1,0:T(8,128)(2,1)S(1)} collective-permute-done((bf16[4,5,16,512]{3,2,1,0:T(8,128)(2,1)S(1)}, bf16[4,5,16,512]{3,2,1,0:T(8,128)(2,1)S(1)}, u32[]{:S(2)}, u32[]{:S(2)}) %collective-permute-start.23) | collective-permute-done | bytes 327712 | tf_op jit(solution)/shard_map/ppermute | solution.py:54
  221.8 2.8 %collective-permute-start.26 = (bf16[5,16,512]{2,1,0:T(8,128)(2,1)S(1)}, bf16[5,16,512]{2,1,0:T(8,128)(2,1)S(1)}, u32[]{:S(2)}, u32[]{:S(2)}) collective-permute-start(bf16[5,16,512]{2,1,0:T(8,128)(2,1)S(1)} %get-tuple-element.155), channel_id=1, source_target_pairs={{0,16},{1,17},{2,18},{3,19},{4,20},{5,21},{6,22},{7,23},{8,24},{9,... | collective-permute-start | bytes 245768 | tf_op jit(solution)/shard_map/ppermute | solution.py:54
  224.7 1.5 collective-permute-start.27
  226.3 3.2 %collective-permute-done.26 = bf16[5,16,512]{2,1,0:T(8,128)(2,1)S(1)} collective-permute-done((bf16[5,16,512]{2,1,0:T(8,128)(2,1)S(1)}, bf16[5,16,512]{2,1,0:T(8,128)(2,1)S(1)}, u32[]{:S(2)}, u32[]{:S(2)}) %collective-permute-start.26) | collective-permute-done | bytes 81952 | tf_op jit(solution)/shard_map/ppermute | solution.py:54
  229.5 1.6 collective-permute-done.27
  237.7 2.6 collective-permute-start.29
  242.0 2.8 %collective-permute-start.30 = (f32[]{:T(128)}, f32[]{:T(128)}, u32[]{:S(2)}, u32[]{:S(2)}) collective-permute-start(f32[]{:T(128)} %add.480), channel_id=1, source_target_pairs={{0,4},{1,5},{2,6},{3,7},{4,0},{5,1},{6,2},{7,3},{8,12},{9,13},{10,... | collective-permute-start | bytes 20 | tf_op jit(solution)/shard_map/ppermute | solution.py:54
  246.3 2.1 collective-permute-start.31
  248.4 1.6 collective-permute-done.31
  250.6 2.7 %collective-permute-start.32 = (f32[]{:T(128)}, f32[]{:T(128)}, u32[]{:S(2)}, u32[]{:S(2)}) collective-permute-start(f32[]{:T(128)} %add.482), channel_id=1, source_target_pairs={{0,16},{1,17},{2,18},{3,19},{4,20},{5,21},{6,22},{7,23},{8,24},{9,... | collective-permute-start | bytes 20 | tf_op jit(solution)/shard_map/ppermute | solution.py:54
  253.3 1.9 collective-permute-done.32
  (247 shorter events, 40.4 us)
Async XLA Ops:
  4.2 7.6 %collective-permute-start = (bf16[6,16,512]{2,1,0:T(8,128)(2,1)S(1)}, bf16[6,16,512]{2,1,0:T(8,128)(2,1)S(1)}, u32[]{:S(2)}, u32[]{:S(2)}) collective-permute-start(bf16[6,16,512]{2,1,0:T(8,128)(2,1)S(1)} %get-tuple-element.163), channel_id=1, source_target_pairs={{0,8},{1,9},{2,10},{3,11},{4,12},{5,13},{6,14},{7,15},{8,0},{9,1},... | collective-permute-start | bytes 294920 | tf_op jit(solution)/shard_map/ppermute | solution.py:54
  7.3 10.4 %collective-permute-start.1 = (bf16[6,16,512]{2,1,0:T(8,128)(2,1)S(1)}, bf16[6,16,512]{2,1,0:T(8,128)(2,1)S(1)}, u32[]{:S(2)}, u32[]{:S(2)}) collective-permute-start(bf16[6,16,512]{2,1,0:T(8,128)(2,1)S(1)} %get-tuple-element.163), channel_id=1, source_target_pairs={{0,16},{1,17},{2,18},{3,19},{4,20},{5,21},{6,22},{7,23},{8,24},{9,... | collective-permute-start | bytes 294920 | tf_op jit(solution)/shard_map/ppermute | solution.py:54
  9.9 7.8 %collective-permute-start.2 = (bf16[6,16,512]{2,1,0:T(8,128)(2,1)S(1)}, bf16[6,16,512]{2,1,0:T(8,128)(2,1)S(1)}, u32[]{:S(2)}, u32[]{:S(2)}) collective-permute-start(bf16[6,16,512]{2,1,0:T(8,128)(2,1)S(1)} %get-tuple-element.163), channel_id=1, source_target_pairs={{0,24},{1,25},{2,26},{3,27},{4,28},{5,29},{6,30},{7,31},{8,16},{9,... | collective-permute-start | bytes 294920 | tf_op jit(solution)/shard_map/ppermute | solution.py:54
  17.8 22.2 %copy-start.10 = (bf16[4,6,16,512]{3,2,1,0:T(8,128)(2,1)}, bf16[4,6,16,512]{3,2,1,0:T(8,128)(2,1)S(1)}, u32[]{:S(2)}) copy-start(bf16[4,6,16,512]{3,2,1,0:T(8,128)(2,1)S(1)} %pad_maximum_fusion.3.refs_0_) | copy-start | bytes 1179652
  17.8 6.6 %collective-permute-start.3 = (bf16[9,16,512]{2,1,0:T(8,128)(2,1)S(1)}, bf16[9,16,512]{2,1,0:T(8,128)(2,1)S(1)}, u32[]{:S(2)}, u32[]{:S(2)}) collective-permute-start(bf16[9,16,512]{2,1,0:T(8,128)(2,1)S(1)} %constant_dynamic-update-slice_fusion), channel_id=1, source_target_pairs={{0,8},{1,9},{2,10},{3,11},{4,12},{5,13},{6,14},{7,15},{8,0},{9,1},... | collective-permute-start | bytes 442376 | tf_op jit(solution)/shard_map/ppermute | solution.py:54
  19.5 15.3 %collective-permute-start.6 = (bf16[4,6,16,512]{3,2,1,0:T(8,128)(2,1)S(1)}, bf16[4,6,16,512]{3,2,1,0:T(8,128)(2,1)S(1)}, u32[]{:S(2)}, u32[]{:S(2)}) collective-permute-start(bf16[4,6,16,512]{3,2,1,0:T(8,128)(2,1)S(1)} %pad_maximum_fusion.3.refs_0_), channel_id=1, source_target_pairs={{0,2},{1,3},{2,0},{3,1},{4,6},{5,7},{6,4},{7,5},{8,10},{9,11},{10,... | collective-permute-start | bytes 1179656 | tf_op jit(solution)/shard_map/ppermute | solution.py:54
  21.0 17.6 %collective-permute-start.7 = (bf16[4,6,16,512]{3,2,1,0:T(8,128)(2,1)S(1)}, bf16[4,6,16,512]{3,2,1,0:T(8,128)(2,1)S(1)}, u32[]{:S(2)}, u32[]{:S(2)}) collective-permute-start(bf16[4,6,16,512]{3,2,1,0:T(8,128)(2,1)S(1)} %pad_maximum_fusion.3.refs_0_), channel_id=1, source_target_pairs={{0,4},{1,5},{2,6},{3,7},{4,0},{5,1},{6,2},{7,3},{8,12},{9,13},{10,... | collective-permute-start | bytes 1179656 | tf_op jit(solution)/shard_map/ppermute | solution.py:54
  22.5 16.1 %collective-permute-start.8 = (bf16[4,6,16,512]{3,2,1,0:T(8,128)(2,1)S(1)}, bf16[4,6,16,512]{3,2,1,0:T(8,128)(2,1)S(1)}, u32[]{:S(2)}, u32[]{:S(2)}) collective-permute-start(bf16[4,6,16,512]{3,2,1,0:T(8,128)(2,1)S(1)} %pad_maximum_fusion.3.refs_0_), channel_id=1, source_target_pairs={{0,6},{1,7},{2,4},{3,5},{4,2},{5,3},{6,0},{7,1},{8,14},{9,15},{10,... | collective-permute-start | bytes 1179656 | tf_op jit(solution)/shard_map/ppermute | solution.py:54
  23.0 11.7 %collective-permute-start.4 = (bf16[9,16,512]{2,1,0:T(8,128)(2,1)S(1)}, bf16[9,16,512]{2,1,0:T(8,128)(2,1)S(1)}, u32[]{:S(2)}, u32[]{:S(2)}) collective-permute-start(bf16[9,16,512]{2,1,0:T(8,128)(2,1)S(1)} %constant_dynamic-update-slice_fusion), channel_id=1, source_target_pairs={{0,16},{1,17},{2,18},{3,19},{4,20},{5,21},{6,22},{7,23},{8,24},{9,... | collective-permute-start | bytes 442376 | tf_op jit(solution)/shard_map/ppermute | solution.py:54
  24.4 10.3 %collective-permute-start.5 = (bf16[9,16,512]{2,1,0:T(8,128)(2,1)S(1)}, bf16[9,16,512]{2,1,0:T(8,128)(2,1)S(1)}, u32[]{:S(2)}, u32[]{:S(2)}) collective-permute-start(bf16[9,16,512]{2,1,0:T(8,128)(2,1)S(1)} %constant_dynamic-update-slice_fusion), channel_id=1, source_target_pairs={{0,24},{1,25},{2,26},{3,27},{4,28},{5,29},{6,30},{7,31},{8,16},{9,... | collective-permute-start | bytes 442376 | tf_op jit(solution)/shard_map/ppermute | solution.py:54
  34.7 5.3 %copy-start.53 = (s32[1024]{0:T(1024)S(1)}, s32[1024]{0:T(1024)}, u32[]{:S(2)}) copy-start(s32[1024]{0:T(1024)} %param.23) | copy-start | bytes 12292
  34.8 37.9 %copy-start.8 = (bf16[4,9,16,512]{3,2,1,0:T(8,128)(2,1)}, bf16[4,9,16,512]{3,2,1,0:T(8,128)(2,1)S(1)}, u32[]{:S(2)}) copy-start(bf16[4,9,16,512]{3,2,1,0:T(8,128)(2,1)S(1)} %pad_maximum_fusion.2.refs_0_) | copy-start | bytes 1769476
  34.8 6.3 %copy-start.54 = (s32[1024]{0:T(1024)S(1)}, s32[1024]{0:T(1024)}, u32[]{:S(2)}) copy-start(s32[1024]{0:T(1024)} %param.24) | copy-start | bytes 12292
  34.8 7.3 %copy-start = (bf16[1024,512]{1,0:T(8,128)(2,1)S(1)}, bf16[1024,512]{1,0:T(8,128)(2,1)}, u32[]{:S(2)}) copy-start(bf16[1024,512]{1,0:T(8,128)(2,1)} %param.22) | copy-start | bytes 3145732
  34.8 5.2 %copy-start.26 = (bf16[4,6,16,512]{3,2,1,0:T(8,128)(2,1)}, bf16[4,6,16,512]{3,2,1,0:T(8,128)(2,1)S(1)}, u32[]{:S(2)}) copy-start(bf16[4,6,16,512]{3,2,1,0:T(8,128)(2,1)S(1)} %collective-permute-done.6.refs_1_) | copy-start | bytes 1179652
  40.0 6.4 %collective-permute-start.9 = (bf16[16,6,16,512]{3,2,1,0:T(8,128)(2,1)}, bf16[16,6,16,512]{3,2,1,0:T(8,128)(2,1)}, u32[]{:S(2)}, u32[]{:S(2)}) collective-permute-start(bf16[16,6,16,512]{3,2,1,0:T(8,128)(2,1)} %pad_maximum_fusion.1), channel_id=1, source_target_pairs={{0,1},{1,0},{2,3},{3,2},{4,5},{5,4},{6,7},{7,6},{8,9},{9,8},{10,11... | collective-permute-start | bytes 4718600 | tf_op jit(solution)/shard_map/ppermute | solution.py:54
  42.9 29.7 %collective-permute-start.10 = (bf16[4,9,16,512]{3,2,1,0:T(8,128)(2,1)S(1)}, bf16[4,9,16,512]{3,2,1,0:T(8,128)(2,1)S(1)}, u32[]{:S(2)}, u32[]{:S(2)}) collective-permute-start(bf16[4,9,16,512]{3,2,1,0:T(8,128)(2,1)S(1)} %pad_maximum_fusion.2.refs_0_), channel_id=1, source_target_pairs={{0,2},{1,3},{2,0},{3,1},{4,6},{5,7},{6,4},{7,5},{8,10},{9,11},{10,... | collective-permute-start | bytes 1769480 | tf_op jit(solution)/shard_map/ppermute | solution.py:54
  44.2 28.5 %collective-permute-start.11 = (bf16[4,9,16,512]{3,2,1,0:T(8,128)(2,1)S(1)}, bf16[4,9,16,512]{3,2,1,0:T(8,128)(2,1)S(1)}, u32[]{:S(2)}, u32[]{:S(2)}) collective-permute-start(bf16[4,9,16,512]{3,2,1,0:T(8,128)(2,1)S(1)} %pad_maximum_fusion.2.refs_0_), channel_id=1, source_target_pairs={{0,4},{1,5},{2,6},{3,7},{4,0},{5,1},{6,2},{7,3},{8,12},{9,13},{10,... | collective-permute-start | bytes 1769480 | tf_op jit(solution)/shard_map/ppermute | solution.py:54
  45.0 27.6 %collective-permute-start.12 = (bf16[4,9,16,512]{3,2,1,0:T(8,128)(2,1)S(1)}, bf16[4,9,16,512]{3,2,1,0:T(8,128)(2,1)S(1)}, u32[]{:S(2)}, u32[]{:S(2)}) collective-permute-start(bf16[4,9,16,512]{3,2,1,0:T(8,128)(2,1)S(1)} %pad_maximum_fusion.2.refs_0_), channel_id=1, source_target_pairs={{0,6},{1,7},{2,4},{3,5},{4,2},{5,3},{6,0},{7,1},{8,14},{9,15},{10,... | collective-permute-start | bytes 1769480 | tf_op jit(solution)/shard_map/ppermute | solution.py:54
  73.8 4.8 %collective-permute-start.13 = (bf16[16,9,16,512]{3,2,1,0:T(8,128)(2,1)S(1)}, bf16[16,9,16,512]{3,2,1,0:T(8,128)(2,1)}, u32[]{:S(2)}, u32[]{:S(2)}) collective-permute-start(bf16[16,9,16,512]{3,2,1,0:T(8,128)(2,1)S(1)} %pad_maximum_fusion), channel_id=1, source_target_pairs={{0,1},{1,0},{2,3},{3,2},{4,5},{5,4},{6,7},{7,6},{8,9},{9,8},{10,11... | collective-permute-start | bytes 7077896 | tf_op jit(solution)/shard_map/ppermute | solution.py:54
  83.5 4.4 %copy-start.34 = (bf16[1024,512]{1,0:T(8,128)(2,1)S(1)}, bf16[1024,512]{1,0:T(8,128)(2,1)}, u32[]{:S(2)}) copy-start(bf16[1024,512]{1,0:T(8,128)(2,1)} %add_convert_fusion.1) | copy-start | bytes 3145732
  83.5 4.4 %copy-start.36 = (bf16[1,32,16,512]{3,2,1,0:T(8,128)(2,1)S(1)}, bf16[1,32,16,512]{3,2,1,0:T(8,128)(2,1)}, u32[]{:S(2)}) copy-start(bf16[1,32,16,512]{3,2,1,0:T(8,128)(2,1)} %get-tuple-element.75) | copy-start | bytes 1572868
  120.3 19.4 %collective-permute-start.14 = (bf16[16,10,16,512]{3,2,1,0:T(8,128)(2,1)}, bf16[16,10,16,512]{3,2,1,0:T(8,128)(2,1)}, u32[]{:S(2)}, u32[]{:S(2)}) collective-permute-start(bf16[16,10,16,512]{3,2,1,0:T(8,128)(2,1)} %get-tuple-element.78), channel_id=1, source_target_pairs={{0,1},{1,0},{2,3},{3,2},{4,5},{5,4},{6,7},{7,6},{8,9},{9,8},{10,11... | collective-permute-start | bytes 7864328 | tf_op jit(solution)/shard_map/ppermute | solution.py:54
  162.9 4.3 %copy-start.9 = (bf16[1024,512]{1,0:T(8,128)(2,1)S(1)}, bf16[1024,512]{1,0:T(8,128)(2,1)}, u32[]{:S(2)}) copy-start(bf16[1024,512]{1,0:T(8,128)(2,1)} %get-tuple-element.132) | copy-start | bytes 3145732
  162.9 4.3 %copy-start.19 = (bf16[1,32,16,512]{3,2,1,0:T(8,128)(2,1)S(1)}, bf16[1,32,16,512]{3,2,1,0:T(8,128)(2,1)}, u32[]{:S(2)}) copy-start(bf16[1,32,16,512]{3,2,1,0:T(8,128)(2,1)} %get-tuple-element.152) | copy-start | bytes 1572868
  163.7 18.0 %collective-permute-start.15 = (bf16[4,10,16,512]{3,2,1,0:T(8,128)(2,1)}, bf16[4,10,16,512]{3,2,1,0:T(8,128)(2,1)}, u32[]{:S(2)}, u32[]{:S(2)}) collective-permute-start(bf16[4,10,16,512]{3,2,1,0:T(8,128)(2,1)} %get-tuple-element.139), channel_id=1, source_target_pairs={{0,2},{1,3},{2,0},{3,1},{4,6},{5,7},{6,4},{7,5},{8,10},{9,11},{10,... | collective-permute-start | bytes 1966088 | tf_op jit(solution)/shard_map/ppermute | solution.py:54
  164.9 29.6 %collective-permute-start.16 = (bf16[4,10,16,512]{3,2,1,0:T(8,128)(2,1)}, bf16[4,10,16,512]{3,2,1,0:T(8,128)(2,1)}, u32[]{:S(2)}, u32[]{:S(2)}) collective-permute-start(bf16[4,10,16,512]{3,2,1,0:T(8,128)(2,1)} %get-tuple-element.138), channel_id=1, source_target_pairs={{0,4},{1,5},{2,6},{3,7},{4,0},{5,1},{6,2},{7,3},{8,12},{9,13},{10,... | collective-permute-start | bytes 1966088 | tf_op jit(solution)/shard_map/ppermute | solution.py:54
  165.8 30.4 %collective-permute-start.17 = (bf16[4,10,16,512]{3,2,1,0:T(8,128)(2,1)}, bf16[4,10,16,512]{3,2,1,0:T(8,128)(2,1)}, u32[]{:S(2)}, u32[]{:S(2)}) collective-permute-start(bf16[4,10,16,512]{3,2,1,0:T(8,128)(2,1)} %get-tuple-element.137), channel_id=1, source_target_pairs={{0,6},{1,7},{2,4},{3,5},{4,2},{5,3},{6,0},{7,1},{8,14},{9,15},{10,... | collective-permute-start | bytes 1966088 | tf_op jit(solution)/shard_map/ppermute | solution.py:54
  196.1 6.6 %collective-permute-start.21 = (bf16[16,5,16,512]{3,2,1,0:T(8,128)(2,1)}, bf16[16,5,16,512]{3,2,1,0:T(8,128)(2,1)}, u32[]{:S(2)}, u32[]{:S(2)}) collective-permute-start(bf16[16,5,16,512]{3,2,1,0:T(8,128)(2,1)} %get-tuple-element.100), channel_id=1, source_target_pairs={{0,1},{1,0},{2,3},{3,2},{4,5},{5,4},{6,7},{7,6},{8,9},{9,8},{10,11... | collective-permute-start | bytes 3932168 | tf_op jit(solution)/shard_map/ppermute | solution.py:54
  196.1 6.6 %copy-start.29 = (bf16[16,5,16,512]{3,2,1,0:T(8,128)(2,1)S(1)}, bf16[16,5,16,512]{3,2,1,0:T(8,128)(2,1)}, u32[]{:S(2)}) copy-start(bf16[16,5,16,512]{3,2,1,0:T(8,128)(2,1)} %get-tuple-element.99) | copy-start | bytes 3932164
  198.2 9.7 %collective-permute-start.18 = (bf16[10,16,512]{2,1,0:T(8,128)(2,1)S(1)}, bf16[10,16,512]{2,1,0:T(8,128)(2,1)S(1)}, u32[]{:S(2)}, u32[]{:S(2)}) collective-permute-start(bf16[10,16,512]{2,1,0:T(8,128)(2,1)S(1)} %get-tuple-element.141), channel_id=1, source_target_pairs={{0,8},{1,9},{2,10},{3,11},{4,12},{5,13},{6,14},{7,15},{8,0},{9,1},... | collective-permute-start | bytes 491528 | tf_op jit(solution)/shard_map/ppermute | solution.py:54
  198.7 15.0 %collective-permute-start.19 = (bf16[10,16,512]{2,1,0:T(8,128)(2,1)S(1)}, bf16[10,16,512]{2,1,0:T(8,128)(2,1)S(1)}, u32[]{:S(2)}, u32[]{:S(2)}) collective-permute-start(bf16[10,16,512]{2,1,0:T(8,128)(2,1)S(1)} %get-tuple-element.143), channel_id=1, source_target_pairs={{0,16},{1,17},{2,18},{3,19},{4,20},{5,21},{6,22},{7,23},{8,24},{9,... | collective-permute-start | bytes 491528 | tf_op jit(solution)/shard_map/ppermute | solution.py:54
  201.3 8.4 %copy-start.2 = (f32[1024,512]{1,0:T(8,128)S(1)}, f32[1024,512]{1,0:T(8,128)}, u32[]{:S(2)}) copy-start(f32[1024,512]{1,0:T(8,128)} %copy-done.1) | copy-start | bytes 6291460
  201.3 8.4 %copy-start.5 = (f32[1024,512]{1,0:T(8,128)S(1)}, f32[1024,512]{1,0:T(8,128)}, u32[]{:S(2)}) copy-start(f32[1024,512]{1,0:T(8,128)} %get-tuple-element.175) | copy-start | bytes 6291460
  201.4 12.4 %collective-permute-start.20 = (bf16[10,16,512]{2,1,0:T(8,128)(2,1)S(1)}, bf16[10,16,512]{2,1,0:T(8,128)(2,1)S(1)}, u32[]{:S(2)}, u32[]{:S(2)}) collective-permute-start(bf16[10,16,512]{2,1,0:T(8,128)(2,1)S(1)} %get-tuple-element.142), channel_id=1, source_target_pairs={{0,24},{1,25},{2,26},{3,27},{4,28},{5,29},{6,30},{7,31},{8,16},{9,... | collective-permute-start | bytes 491528 | tf_op jit(solution)/shard_map/ppermute | solution.py:54
  204.5 11.3 %collective-permute-start.22 = (bf16[4,5,16,512]{3,2,1,0:T(8,128)(2,1)S(1)}, bf16[4,5,16,512]{3,2,1,0:T(8,128)(2,1)S(1)}, u32[]{:S(2)}, u32[]{:S(2)}) collective-permute-start(bf16[4,5,16,512]{3,2,1,0:T(8,128)(2,1)S(1)} %get-tuple-element.145), channel_id=1, source_target_pairs={{0,2},{1,3},{2,0},{3,1},{4,6},{5,7},{6,4},{7,5},{8,10},{9,11},{10,... | collective-permute-start | bytes 983048 | tf_op jit(solution)/shard_map/ppermute | solution.py:54
  205.4 16.2 %collective-permute-start.23 = (bf16[4,5,16,512]{3,2,1,0:T(8,128)(2,1)S(1)}, bf16[4,5,16,512]{3,2,1,0:T(8,128)(2,1)S(1)}, u32[]{:S(2)}, u32[]{:S(2)}) collective-permute-start(bf16[4,5,16,512]{3,2,1,0:T(8,128)(2,1)S(1)} %get-tuple-element.147), channel_id=1, source_target_pairs={{0,4},{1,5},{2,6},{3,7},{4,0},{5,1},{6,2},{7,3},{8,12},{9,13},{10,... | collective-permute-start | bytes 983048 | tf_op jit(solution)/shard_map/ppermute | solution.py:54
  208.0 13.6 %collective-permute-start.24 = (bf16[4,5,16,512]{3,2,1,0:T(8,128)(2,1)S(1)}, bf16[4,5,16,512]{3,2,1,0:T(8,128)(2,1)S(1)}, u32[]{:S(2)}, u32[]{:S(2)}) collective-permute-start(bf16[4,5,16,512]{3,2,1,0:T(8,128)(2,1)S(1)} %get-tuple-element.146), channel_id=1, source_target_pairs={{0,6},{1,7},{2,4},{3,5},{4,2},{5,3},{6,0},{7,1},{8,14},{9,15},{10,... | collective-permute-start | bytes 983048 | tf_op jit(solution)/shard_map/ppermute | solution.py:54
  215.7 40.2 %copy-start.59 = (f32[64]{0:T(128)S(1)}, f32[64]{0:T(128)}, u32[]{:S(2)}) copy-start(f32[64]{0:T(128)} %param.41) | copy-start | bytes 772
  215.7 40.2 %copy-start.60 = (f32[64]{0:T(128)S(1)}, f32[64]{0:T(128)}, u32[]{:S(2)}) copy-start(f32[64]{0:T(128)} %param.42) | copy-start | bytes 772
  215.7 40.3 %copy-start.61 = (f32[64]{0:T(128)S(1)}, f32[64]{0:T(128)}, u32[]{:S(2)}) copy-start(f32[64]{0:T(128)} %param.43) | copy-start | bytes 772
  215.7 40.9 %copy-start.55 = (f32[7,16]{1,0:T(8,128)S(1)}, f32[7,16]{1,0:T(8,128)}, u32[]{:S(2)}) copy-start(f32[7,16]{1,0:T(8,128)} %param.38) | copy-start | bytes 1348
  215.7 40.9 %copy-start.57 = (f32[7,16]{1,0:T(8,128)S(1)}, f32[7,16]{1,0:T(8,128)}, u32[]{:S(2)}) copy-start(f32[7,16]{1,0:T(8,128)} %param.39) | copy-start | bytes 1348
  215.7 40.9 %copy-start.58 = (f32[7,16]{1,0:T(8,128)S(1)}, f32[7,16]{1,0:T(8,128)}, u32[]{:S(2)}) copy-start(f32[7,16]{1,0:T(8,128)} %param.40) | copy-start | bytes 1348
  215.7 41.6 %copy-start.37 = (f32[64,512]{1,0:T(8,128)S(1)}, f32[64,512]{1,0:T(8,128)}, u32[]{:S(2)}) copy-start(f32[64,512]{1,0:T(8,128)} %param.35) | copy-start | bytes 393220
  215.7 41.6 %copy-start.45 = (f32[64,512]{1,0:T(8,128)S(1)}, f32[64,512]{1,0:T(8,128)}, u32[]{:S(2)}) copy-start(f32[64,512]{1,0:T(8,128)} %param.36) | copy-start | bytes 393220
  215.7 41.5 %copy-start.46 = (f32[64,512]{1,0:T(8,128)S(1)}, f32[64,512]{1,0:T(8,128)}, u32[]{:S(2)}) copy-start(f32[64,512]{1,0:T(8,128)} %param.37) | copy-start | bytes 393220
  221.6 36.5 %copy-start.44 = (f32[2,16,512]{2,1,0:T(8,128)S(1)}, f32[2,16,512]{2,1,0:T(8,128)}, u32[]{:S(2)}) copy-start(f32[2,16,512]{2,1,0:T(8,128)} %param.29) | copy-start | bytes 196612
  221.6 36.5 %copy-start.51 = (f32[2,16,512]{2,1,0:T(8,128)S(1)}, f32[2,16,512]{2,1,0:T(8,128)}, u32[]{:S(2)}) copy-start(f32[2,16,512]{2,1,0:T(8,128)} %param.30) | copy-start | bytes 196612
  221.6 36.5 %copy-start.52 = (f32[2,16,512]{2,1,0:T(8,128)S(1)}, f32[2,16,512]{2,1,0:T(8,128)}, u32[]{:S(2)}) copy-start(f32[2,16,512]{2,1,0:T(8,128)} %param.31) | copy-start | bytes 196612
  221.6 37.2 %copy-start.38 = (f32[4,16,512]{2,1,0:T(8,128)S(1)}, f32[4,16,512]{2,1,0:T(8,128)}, u32[]{:S(2)}) copy-start(f32[4,16,512]{2,1,0:T(8,128)} %param.26) | copy-start | bytes 393220
  221.6 37.2 %copy-start.47 = (f32[4,16,512]{2,1,0:T(8,128)S(1)}, f32[4,16,512]{2,1,0:T(8,128)}, u32[]{:S(2)}) copy-start(f32[4,16,512]{2,1,0:T(8,128)} %param.27) | copy-start | bytes 393220
  221.6 37.2 %copy-start.48 = (f32[4,16,512]{2,1,0:T(8,128)S(1)}, f32[4,16,512]{2,1,0:T(8,128)}, u32[]{:S(2)}) copy-start(f32[4,16,512]{2,1,0:T(8,128)} %param.28) | copy-start | bytes 393220
  221.8 4.5 %collective-permute-start.25 = (bf16[5,16,512]{2,1,0:T(8,128)(2,1)S(1)}, bf16[5,16,512]{2,1,0:T(8,128)(2,1)S(1)}, u32[]{:S(2)}, u32[]{:S(2)}) collective-permute-start(bf16[5,16,512]{2,1,0:T(8,128)(2,1)S(1)} %get-tuple-element.153), channel_id=1, source_target_pairs={{0,8},{1,9},{2,10},{3,11},{4,12},{5,13},{6,14},{7,15},{8,0},{9,1},... | collective-permute-start | bytes 245768 | tf_op jit(solution)/shard_map/ppermute | solution.py:54
  221.8 7.6 %collective-permute-start.26 = (bf16[5,16,512]{2,1,0:T(8,128)(2,1)S(1)}, bf16[5,16,512]{2,1,0:T(8,128)(2,1)S(1)}, u32[]{:S(2)}, u32[]{:S(2)}) collective-permute-start(bf16[5,16,512]{2,1,0:T(8,128)(2,1)S(1)} %get-tuple-element.155), channel_id=1, source_target_pairs={{0,16},{1,17},{2,18},{3,19},{4,20},{5,21},{6,22},{7,23},{8,24},{9,... | collective-permute-start | bytes 245768 | tf_op jit(solution)/shard_map/ppermute | solution.py:54
  224.7 6.3 %collective-permute-start.27 = (bf16[5,16,512]{2,1,0:T(8,128)(2,1)S(1)}, bf16[5,16,512]{2,1,0:T(8,128)(2,1)S(1)}, u32[]{:S(2)}, u32[]{:S(2)}) collective-permute-start(bf16[5,16,512]{2,1,0:T(8,128)(2,1)S(1)} %get-tuple-element.154), channel_id=1, source_target_pairs={{0,24},{1,25},{2,26},{3,27},{4,28},{5,29},{6,30},{7,31},{8,16},{9,... | collective-permute-start | bytes 245768 | tf_op jit(solution)/shard_map/ppermute | solution.py:54
  226.2 33.4 %copy-start.39 = (f32[16,2048]{1,0:T(8,128)S(1)}, f32[16,2048]{1,0:T(8,128)}, u32[]{:S(2)}) copy-start(f32[16,2048]{1,0:T(8,128)} %param.32) | copy-start | bytes 393220
  226.2 33.4 %copy-start.49 = (f32[16,2048]{1,0:T(8,128)S(1)}, f32[16,2048]{1,0:T(8,128)}, u32[]{:S(2)}) copy-start(f32[16,2048]{1,0:T(8,128)} %param.33) | copy-start | bytes 393220
  226.2 33.4 %copy-start.50 = (f32[16,2048]{1,0:T(8,128)S(1)}, f32[16,2048]{1,0:T(8,128)}, u32[]{:S(2)}) copy-start(f32[16,2048]{1,0:T(8,128)} %param.34) | copy-start | bytes 393220
  235.7 1.4 collective-permute-start.28
  237.7 3.7 %collective-permute-start.29 = (f32[]{:T(128)}, f32[]{:T(128)}, u32[]{:S(2)}, u32[]{:S(2)}) collective-permute-start(f32[]{:T(128)} %add.479), channel_id=1, source_target_pairs={{0,2},{1,3},{2,0},{3,1},{4,6},{5,7},{6,4},{7,5},{8,10},{9,11},{10,... | collective-permute-start | bytes 20 | tf_op jit(solution)/shard_map/ppermute | solution.py:54
  242.0 3.7 %collective-permute-start.30 = (f32[]{:T(128)}, f32[]{:T(128)}, u32[]{:S(2)}, u32[]{:S(2)}) collective-permute-start(f32[]{:T(128)} %add.480), channel_id=1, source_target_pairs={{0,4},{1,5},{2,6},{3,7},{4,0},{5,1},{6,2},{7,3},{8,12},{9,13},{10,... | collective-permute-start | bytes 20 | tf_op jit(solution)/shard_map/ppermute | solution.py:54
  246.3 3.7 %collective-permute-start.31 = (f32[]{:T(128)}, f32[]{:T(128)}, u32[]{:S(2)}, u32[]{:S(2)}) collective-permute-start(f32[]{:T(128)} %add.481), channel_id=1, source_target_pairs={{0,8},{1,9},{2,10},{3,11},{4,12},{5,13},{6,14},{7,15},{8,0},{9,1},... | collective-permute-start | bytes 20 | tf_op jit(solution)/shard_map/ppermute | solution.py:54
  250.6 4.6 %collective-permute-start.32 = (f32[]{:T(128)}, f32[]{:T(128)}, u32[]{:S(2)}, u32[]{:S(2)}) collective-permute-start(f32[]{:T(128)} %add.482), channel_id=1, source_target_pairs={{0,16},{1,17},{2,18},{3,19},{4,20},{5,21},{6,22},{7,23},{8,24},{9,... | collective-permute-start | bytes 20 | tf_op jit(solution)/shard_map/ppermute | solution.py:54
  (33 other events, 64.9 us)
